TPU v7x, 512 devices: a whole 4x4x16 slice. The times are simulated.
512 devices in a mesh: depth: 32 (over x, y, core), height: 16 (over z).
Axes of the slice: x: 4, y: 4, z: 16, core: 2. Of those that a mesh axis runs over, the one named last changes fastest.
Arguments:
- middle_input: bfloat16 [64, 32, 64, 128], P('depth', None, 'height'), may hold values from -6 to 6
- middle_cotangent: bfloat16 [64, 32, 64, 128], P('depth', None, 'height'), may hold values from -6 to 6
- middle_weight: bfloat16 [3, 3, 3, 32, 32], replicated, may hold values from -0.21875 to 0.21875
- coarse_input: bfloat16 [32, 32, 64, 128], P('depth', 'height'), may hold values from -6 to 6
- coarse_cotangent: bfloat16 [32, 32, 64, 128], P('depth', 'height'), may hold values from -6 to 6
- coarse_weight: bfloat16 [3, 3, 3, 128, 128], P(None, None, None, None, 'depth'), may hold values from -0.109375 to 0.109375
Outputs:
- middle_output: bfloat16 [64, 32, 64, 128], P('depth', None, 'height')
- middle_input_grad: bfloat16 [64, 32, 64, 128], P('depth', None, 'height')
- middle_weight_grad: float32 [3, 3, 3, 32, 32], replicated
- coarse_output: bfloat16 [32, 32, 64, 128], P('depth', 'height')
- coarse_input_grad: bfloat16 [32, 32, 64, 128], P('depth', 'height')
- coarse_weight_grad: float32 [3, 3, 3, 128, 128], P(None, None, None, None, 'depth')
All inputs are finite; a program needn't handle non-finite values.
Results may differ from a plain program's by a relative error of at most 0.001.
Values may be sent and summed in bfloat16 or wider, within the bound.
A program may use at most 64 MiB of HBM per device.

v0:
```python
import math

import jax
import jax.numpy as jnp
from jax import lax
from jax.sharding import Mesh
from jax.sharding import PartitionSpec as P

DEPTH = ("depth_0", "depth_1", "depth_2")


def padded_2(x, sides, width):
    for axis, dim in sides:
        peers, length = (lax.axis_size(axis), x.shape[dim])
        up = [(i, (i + 1) % peers) for i in range(peers - 1)]
        down = [(j, i) for i, j in up]
        last = lax.slice_in_dim(x, length - width, length, axis=dim)
        leading = lax.slice_in_dim(x, 0, width, axis=dim)
        before = lax.ppermute(last, axis, up)
        after = lax.ppermute(leading, axis, down)
        x = jnp.concatenate([before, x, after], axis=dim)
    return x


def sent_to_all(x, axis):
    peers = lax.axis_size(axis)
    return lax.all_to_all(jnp.broadcast_to(x[None], (peers, *x.shape)), axis, 0, 0, tiled=True)


def joined_along(pieces, dim):
    lengths = list(pieces.shape[1:])
    lengths[dim] *= pieces.shape[0]
    return jnp.moveaxis(pieces, 0, dim).reshape(lengths)


def gather_directly(x, axis, dim):
    pieces = sent_to_all(x, axis)
    return joined_along(pieces, dim)


def padded_to(lines, peers):
    spare = -len(lines) % peers
    return jnp.pad(lines, [(0, spare)] + [(0, 0)] * (lines.ndim - 1))


def whole_of(x, axes, dim):
    far, near = axes
    pieces = sent_to_all(sent_to_all(x, far), near)
    return joined_along(pieces.swapaxes(0, 1).reshape(-1, *x.shape), dim)


def cut_along(x, dim, peers):
    before, after = (x.shape[:dim], x.shape[dim + 1 :])
    return jnp.moveaxis(x.reshape(*before, peers, -1, *after), dim, 0)


def sent_and_summed(x, axis, dim):
    pieces = cut_along(x, dim, lax.axis_size(axis))
    arrived = lax.all_to_all(pieces, axis, split_axis=0, concat_axis=0, tiled=True)
    return arrived.sum(axis=0)


def sum_by_axis(x, axes, dim):
    far, near = axes
    own = sent_and_summed(cut_along(x, dim, lax.axis_size(far)), near, dim + 1)
    return jnp.sum(lax.all_to_all(own, far, 0, 0, tiled=True), axis=0)


def sum_by_parts(x, axes):
    padded = padded_to(x, lax.axis_size(axes[0]) * lax.axis_size(axes[1]))
    whole = whole_of(sum_by_axis(padded, axes, 0), axes, 0)
    return lax.slice_in_dim(whole, 0, len(x)).reshape(x.shape)


def together(arrays, axis):
    ends = [0]
    for a in arrays:
        ends.append(ends[-1] + a.size)
    running = sum_by_parts(jnp.concatenate([a.ravel() for a in arrays]), axis)
    return tuple((running[b:e].reshape(a.shape) for a, b, e in zip(arrays, ends, ends[1:])))


def backward_taps(weight):
    flipped = weight[::-1, ::-1, ::-1]
    return jnp.swapaxes(flipped, 3, 4)


def plane_taps(window, offset, amount, height, breadth):
    pieces = []
    for depth_tap in range(3):
        for height_tap in range(3):
            for width_tap in range(3):
                pieces.append(
                    window[
                        depth_tap,
                        offset : offset + amount,
                        height_tap : height_tap + height,
                        width_tap : width_tap + breadth,
                    ]
                )
    stacked = jnp.stack(pieces)
    return stacked.reshape(27 * amount, height * breadth)


def coarse_taps(padded, offset, amount, planes, height, breadth):
    pieces = []
    for depth_tap in range(3):
        for height_tap in range(3):
            for width_tap in range(3):
                pieces.append(
                    padded[
                        depth_tap : depth_tap + planes,
                        height_tap : height_tap + height,
                        width_tap : width_tap + breadth,
                        offset : offset + amount,
                    ]
                )
    stacked = jnp.concatenate(pieces, axis=3)
    return stacked.reshape(planes * height * breadth, 27 * amount)


def level_second(extended, weight):
    channels = weight.shape[3]
    padded = jnp.pad(extended, ((0, 0), (0, 0), (0, 0), (1, 1)))
    planes = padded.shape[0] - 2
    height = padded.shape[2] - 2
    breadth = padded.shape[3] - 2
    forward_matrix = weight.reshape(27 * channels, channels).T
    backward_matrix = backward_taps(weight).reshape(27 * channels, channels).T

    def one_plane(carried, plane_at):
        window = lax.dynamic_slice_in_dim(padded, plane_at, 3, 0)
        source = plane_taps(window, 0, channels, height, breadth)
        upstream = plane_taps(window, channels, channels, height, breadth)
        center = window[1, channels:, 1 : height + 1, 1 : breadth + 1].reshape(
            channels, height * breadth
        )
        output = jnp.dot(forward_matrix, source, preferred_element_type=jnp.float32)
        grad_in = jnp.dot(backward_matrix, upstream, preferred_element_type=jnp.float32)
        carried = carried + lax.dot_general(
            source, center, (((1,), (1,)), ((), ())), preferred_element_type=jnp.float32
        )
        output = output.astype(jnp.bfloat16).reshape(channels, height, breadth)
        grad_in = grad_in.astype(jnp.bfloat16).reshape(channels, height, breadth)
        return (carried, (output, grad_in))

    initial = jnp.zeros((27 * channels, channels), jnp.float32)
    summed, (outputs, gradients) = lax.scan(one_plane, initial, jnp.arange(planes))
    return (outputs, gradients, summed.reshape(3, 3, 3, channels, channels))


def per_device(
    middle_input, middle_cotangent, middle_weight, coarse_input, coarse_cotangent, coarse_weight
):
    middle_cells = (
        middle_input.shape[0]
        * lax.axis_size(DEPTH)
        * middle_input.shape[2]
        * lax.axis_size("height")
        * middle_input.shape[3]
    )
    coarse_cells = (
        coarse_input.shape[0]
        * lax.axis_size(DEPTH)
        * coarse_input.shape[1]
        * lax.axis_size("height")
        * coarse_input.shape[2]
    )
    middle_stack = jnp.concatenate((middle_input, middle_cotangent), axis=1)
    middle_ext = padded_2(middle_stack, ((DEPTH, 0), ("height", 2)), 1)
    middle_out, middle_dx, middle_part = level_second(middle_ext, middle_weight)
    channels = coarse_input.shape[3]
    coarse_stack = jnp.concatenate((coarse_input, coarse_cotangent), axis=3)
    coarse_ext = padded_2(coarse_stack, ((DEPTH, 0), ("height", 1)), 1)
    padded = jnp.pad(coarse_ext, ((0, 0), (0, 0), (1, 1), (0, 0)))
    planes = padded.shape[0] - 2
    height = padded.shape[1] - 2
    breadth = padded.shape[2] - 2
    full_weight = gather_directly(coarse_weight, DEPTH, 4)
    source = coarse_taps(padded, 0, channels, planes, height, breadth)
    upstream = coarse_taps(padded, channels, channels, planes, height, breadth)
    center = padded[1 : planes + 1, 1 : height + 1, 1 : breadth + 1, channels:].reshape(
        planes * height * breadth, channels
    )
    coarse_out = jnp.dot(
        source, full_weight.reshape(27 * channels, channels), preferred_element_type=jnp.float32
    )
    coarse_out = coarse_out.astype(jnp.bfloat16).reshape(planes, height, breadth, channels)
    coarse_dx = jnp.dot(
        upstream,
        backward_taps(full_weight).reshape(27 * channels, channels),
        preferred_element_type=jnp.float32,
    )
    coarse_dx = coarse_dx.astype(jnp.bfloat16).reshape(planes, height, breadth, channels)
    shard_rows = channels // lax.axis_size(DEPTH)
    partial_value = lax.dot_general(
        source, center, (((0,), (0,)), ((), ())), preferred_element_type=jnp.float32
    )
    middle_part, summed = together(
        (middle_part, partial_value), (("depth_0", "depth_1"), ("depth_2", "height"))
    )
    anchor = lax.axis_index(DEPTH) * shard_rows
    coarse_share = lax.dynamic_slice_in_dim(summed, anchor, shard_rows, 1)
    coarse_dw = coarse_share.reshape(3, 3, 3, channels, shard_rows) * (
        1.0 / math.sqrt(coarse_cells)
    )
    middle_dw = middle_part * (1.0 / math.sqrt(middle_cells))
    return (middle_out, middle_dx, middle_dw, coarse_out, coarse_dx, coarse_dw)


def solution(mesh):
    finer = Mesh(
        mesh.devices.reshape(4, 4, 2, mesh.shape["height"]),
        ("depth_0", "depth_1", "depth_2", "height"),
    )
    placed = (
        P(DEPTH, None, "height", None),
        P(DEPTH, None, "height", None),
        P(),
        P(DEPTH, "height", None, None),
        P(DEPTH, "height", None, None),
        P(None, None, None, None, DEPTH),
    )
    return jax.shard_map(
        per_device,
        mesh=finer,
        in_specs=placed,
        out_specs=(
            P(DEPTH, None, "height", None),
            P(DEPTH, None, "height", None),
            P(),
            P(DEPTH, "height", None, None),
            P(DEPTH, "height", None, None),
            P(None, None, None, None, DEPTH),
        ),
        check_vma=False,
    )
```

profile of v0, /device:TPU:1, one launch (start us, length us, event | category | flops | bytes accessed | tf_op | source)
XLA Modules:
  0.0 340.1 jit_solution(12258316196041956526)
XLA Ops:
  0.6 0.8 constant_dynamic-update-slice_fusion.59
  1.4 0.8 constant_dynamic-update-slice_fusion.58
  2.2 8.8 %collective-permute-start.5 = (bf16[1,2,64,256]{3,2,1,0:T(8,128)(2,1)S(1)}, bf16[1,2,64,256]{3,2,1,0:T(8,128)(2,1)S(1)}, u32[]{:S(2)}, u32[]{:S(2)}) collective-permute-start(bf16[1,2,64,256]{3,2,1,0:T(8,128)(2,1)S(1)} %constant_dynamic-update-slice_fusion.58), channel_id=1, source_target_pairs={{16,0},{32,16},{48,32},{64,48},{80,64},{96,80},{112,96},{128,112},... | collective-permute-start | bytes 196616 | tf_op jit(solution)/shard_map/ppermute | solution.py:20
  11.0 1.9 collective-permute-start.4
  12.9 0.9 constant_dynamic-update-slice_fusion.57
  13.8 0.9 constant_dynamic-update-slice_fusion.56
  14.7 1.9 collective-permute-start
  16.6 2.4 collective-permute-start.1
  19.1 1.1 copy.50
  20.1 1.0 reverse_bitcast_fusion
  21.4 0.8 collective-permute-done.1
  22.6 1.3 collective-permute-start.2
  23.9 1.3 collective-permute-start.3
  25.3 4.0 %collective-permute-start.6 = (bf16[3,1,64,256]{3,2,1,0:T(8,128)(2,1)S(1)}, bf16[3,1,64,256]{3,2,1,0:T(8,128)(2,1)S(1)}, u32[]{:S(2)}, u32[]{:S(2)}) collective-permute-start(bf16[3,1,64,256]{3,2,1,0:T(8,128)(2,1)S(1)} %get-tuple-element.203), channel_id=1, source_target_pairs={{0,1},{1,2},{2,3},{3,4},{4,5},{5,6},{6,7},{7,8},{8,9},{9,10},{10,1... | collective-permute-start | bytes 294920 | tf_op jit(solution)/shard_map/ppermute | solution.py:19
  29.3 1.3 collective-permute-start.7
  30.6 1.8 select_maximum_fusion
  32.4 14.2 %while.15 = (s32[]{:T(128)}, f32[864,32]{0,1:T(8,128)S(1)}, bf16[2,32,4,128]{3,2,1,0:T(4,128)(2,1)S(1)}, bf16[2,32,4,128]{3,2,1,0:T(4,128)(2,1)S(1)}, s32[2]{0:T...) while((s32[]{:T(128)}, f32[864,32]{0,1:T(8,128)S(1)}, ...), condition=%wide.region_1.2_spmd.clone, body=%wide.region_0.1_spmd.clone.sunk | while | flops 85022728 | bytes 6918741 | solution.py:148
  32.4 0.6 dynamic_slice.15
  39.5 0.6 dynamic_slice.15
  48.2 1.0 copy-done.3
  49.1 0.9 copy-done.1
  50.0 0.4 convolution_bitcast_fusion
  50.5 1.4 pad_maximum_fusion
  51.9 3.3 reshape_reshape.11
  55.2 1.2 copy.44
  56.4 111.4 %all_to_all.30 = f32[32,16,918]{2,1,0:T(8,128)S(1)} all-to-all(f32[32,16,918]{2,1,0:T(8,128)S(1)} %copy.44), channel_id=1, replica_groups=mesh['depth_0'=4,'depth_1'=4,'depth_2'=2,'height'=16] {'depth_2','height'}, dimensions={0} | all-to-all | bytes 3760128 | tf_op jit(solution)/shard_map/all_to_all | solution.py:59
  168.0 16.5 %all_to_all.31 = f32[16,1,918]{2,1,0:T(1,128)S(1)} all-to-all(f32[16,1,918]{2,1,0:T(1,128)S(1)} %all_to_all.20), channel_id=1, replica_groups=mesh['depth_0'=4,'depth_1'=4,'depth_2'=2,'height'=16] {'depth_0','depth_1'}, dimensions={0} | all-to-all | bytes 117504 | tf_op jit(solution)/shard_map/all_to_all | solution.py:66
  184.6 9.8 %all_to_all.32 = f32[16,1,918]{2,1,0:T(1,128)S(1)} all-to-all(f32[16,1,918]{2,1,0:T(1,128)S(1)} %broadcast_in_dim.31), channel_id=1, replica_groups=mesh['depth_0'=4,'depth_1'=4,'depth_2'=2,'height'=16] {'depth_0','depth_1'}, dimensions={0} | all-to-all | bytes 117504 | tf_op jit(solution)/shard_map/all_to_all | solution.py:27
  194.4 1.2 broadcast_in_dim.34
  195.6 7.7 %all-to-all-start.4 = ((bf16[32,3,3,3,128,4]{4,5,3,2,1,0:T(4,128)(2,1)}), bf16[32,3,3,3,128,4]{4,5,3,2,1,0:T(4,128)(2,1)S(1)}, u32[]{:S(2)}, u32[]{:S(2)}) async-start(bf16[32,3,3,3,128,4]{4,5,3,2,1,0:T(4,128)(2,1)} %broadcast_in_dim.34), calls=%async_computation.4 | async-start | bytes 1769472 | tf_op jit(solution)/shard_map/all_to_all | solution.py:27
  203.3 15.3 %all-to-all-done.4 = bf16[32,3,3,3,128,4]{4,5,3,2,1,0:T(4,128)(2,1)S(1)} async-done(((bf16[32,3,3,3,128,4]{4,5,3,2,1,0:T(4,128)(2,1)}), bf16[32,3,3,3,128,4]{4,5,3,2,1,0:T(4,128)(2,1)S(1)}, u32[]{:S(2)}, u32[]{:S(2)}) %all-to-all-start.4) | async-done | bytes 884768 | tf_op jit(solution)/shard_map/all_to_all | solution.py:27
  218.6 1.6 broadcast_in_dim.33
  220.1 7.4 %all-to-all-start.3 = ((f32[32,16,918]{2,1,0:T(8,128)}), f32[32,16,918]{2,1,0:T(8,128)S(1)}, u32[]{:S(2)}, u32[]{:S(2)}) async-start(f32[32,16,918]{2,1,0:T(8,128)} %broadcast_in_dim.33), calls=%async_computation.3 | async-start | bytes 4194304 | tf_op jit(solution)/shard_map/all_to_all | solution.py:27
  227.5 1.4 copy.47
  228.9 1.5 copy.46
  230.4 2.2 rev.7
  232.6 3.4 reshape_reshape.12
  236.0 2.4 convolution_convert_fusion.2
  238.4 2.2 convolution_convert_fusion.3
  240.6 81.0 %all-to-all-done.3 = f32[32,16,918]{2,1,0:T(8,128)S(1)} async-done(((f32[32,16,918]{2,1,0:T(8,128)}), f32[32,16,918]{2,1,0:T(8,128)S(1)}, u32[]{:S(2)}, u32[]{:S(2)}) %all-to-all-start.3) | async-done | bytes 1880096 | tf_op jit(solution)/shard_map/all_to_all | solution.py:27
  321.7 1.3 copy-done
  323.0 2.8 copy.45
  325.8 2.8 slice.454
  328.6 6.5 %slice.426 = f32[51,3,3,32,32]{4,3,2,1,0:T(8,128)} reshape(f32[16,32,918]{2,1,0:T(8,128)S(1)} %copy.45) | data formatting | bytes 3760128 | tf_op jit(solution)/shard_map/slice | solution.py:80
  335.1 1.5 slice-done
  336.6 0.5 dynamic-slice_multiply_fusion
  337.1 1.2 copy.57
  338.3 1.8 slice_multiply_fusion
  (135 shorter events, 11.3 us)
Async XLA Ops:
  2.2 23.0 %collective-permute-start.5 = (bf16[1,2,64,256]{3,2,1,0:T(8,128)(2,1)S(1)}, bf16[1,2,64,256]{3,2,1,0:T(8,128)(2,1)S(1)}, u32[]{:S(2)}, u32[]{:S(2)}) collective-permute-start(bf16[1,2,64,256]{3,2,1,0:T(8,128)(2,1)S(1)} %constant_dynamic-update-slice_fusion.58), channel_id=1, source_target_pairs={{16,0},{32,16},{48,32},{64,48},{80,64},{96,80},{112,96},{128,112},... | collective-permute-start | bytes 196616 | tf_op jit(solution)/shard_map/ppermute | solution.py:20
  11.0 14.3 %collective-permute-start.4 = (bf16[1,2,64,256]{3,2,1,0:T(8,128)(2,1)S(1)}, bf16[1,2,64,256]{3,2,1,0:T(8,128)(2,1)S(1)}, u32[]{:S(2)}, u32[]{:S(2)}) collective-permute-start(bf16[1,2,64,256]{3,2,1,0:T(8,128)(2,1)S(1)} %constant_dynamic-update-slice_fusion.58), channel_id=1, source_target_pairs={{0,16},{16,32},{32,48},{48,64},{64,80},{80,96},{96,112},{112,128},... | collective-permute-start | bytes 196616 | tf_op jit(solution)/shard_map/ppermute | solution.py:19
  14.7 6.7 %collective-permute-start = (bf16[1,64,4,128]{3,2,1,0:T(4,128)(2,1)S(1)}, bf16[1,64,4,128]{3,2,1,0:T(4,128)(2,1)S(1)}, u32[]{:S(2)}, u32[]{:S(2)}) collective-permute-start(bf16[1,64,4,128]{3,2,1,0:T(4,128)(2,1)S(1)} %get-tuple-element.205), channel_id=1, source_target_pairs={{0,16},{16,32},{32,48},{48,64},{64,80},{80,96},{96,112},{112,128},... | collective-permute-start | bytes 196616 | tf_op jit(solution)/shard_map/ppermute | solution.py:19
  16.6 5.6 %collective-permute-start.1 = (bf16[1,64,4,128]{3,2,1,0:T(4,128)(2,1)S(1)}, bf16[1,64,4,128]{3,2,1,0:T(4,128)(2,1)S(1)}, u32[]{:S(2)}, u32[]{:S(2)}) collective-permute-start(bf16[1,64,4,128]{3,2,1,0:T(4,128)(2,1)S(1)} %get-tuple-element.206), channel_id=1, source_target_pairs={{16,0},{32,16},{48,32},{64,48},{80,64},{96,80},{112,96},{128,112},... | collective-permute-start | bytes 196616 | tf_op jit(solution)/shard_map/ppermute | solution.py:20
  22.6 8.0 %collective-permute-start.2 = (bf16[4,64,1,128]{3,2,1,0:T(2,128)(2,1)S(1)}, bf16[4,64,1,128]{3,2,1,0:T(2,128)(2,1)S(1)}, u32[]{:S(2)}, u32[]{:S(2)}) collective-permute-start(bf16[4,64,1,128]{3,2,1,0:T(2,128)(2,1)S(1)} %get-tuple-element.201), channel_id=1, source_target_pairs={{0,1},{1,2},{2,3},{3,4},{4,5},{5,6},{6,7},{7,8},{8,9},{9,10},{10,1... | collective-permute-start | bytes 196616 | tf_op jit(solution)/shard_map/ppermute | solution.py:19
  23.9 6.7 %collective-permute-start.3 = (bf16[4,64,1,128]{3,2,1,0:T(2,128)(2,1)S(1)}, bf16[4,64,1,128]{3,2,1,0:T(2,128)(2,1)S(1)}, u32[]{:S(2)}, u32[]{:S(2)}) collective-permute-start(bf16[4,64,1,128]{3,2,1,0:T(2,128)(2,1)S(1)} %get-tuple-element.202), channel_id=1, source_target_pairs={{1,0},{2,1},{3,2},{4,3},{5,4},{6,5},{7,6},{8,7},{9,8},{10,9},{11,1... | collective-permute-start | bytes 196616 | tf_op jit(solution)/shard_map/ppermute | solution.py:20
  25.3 21.8 %collective-permute-start.6 = (bf16[3,1,64,256]{3,2,1,0:T(8,128)(2,1)S(1)}, bf16[3,1,64,256]{3,2,1,0:T(8,128)(2,1)S(1)}, u32[]{:S(2)}, u32[]{:S(2)}) collective-permute-start(bf16[3,1,64,256]{3,2,1,0:T(8,128)(2,1)S(1)} %get-tuple-element.203), channel_id=1, source_target_pairs={{0,1},{1,2},{2,3},{3,4},{4,5},{5,6},{6,7},{7,8},{8,9},{9,10},{10,1... | collective-permute-start | bytes 294920 | tf_op jit(solution)/shard_map/ppermute | solution.py:19
  29.3 17.8 %collective-permute-start.7 = (bf16[3,1,64,256]{3,2,1,0:T(8,128)(2,1)S(1)}, bf16[3,1,64,256]{3,2,1,0:T(8,128)(2,1)S(1)}, u32[]{:S(2)}, u32[]{:S(2)}) collective-permute-start(bf16[3,1,64,256]{3,2,1,0:T(8,128)(2,1)S(1)} %get-tuple-element.204), channel_id=1, source_target_pairs={{1,0},{2,1},{3,2},{4,3},{5,4},{6,5},{7,6},{8,7},{9,8},{10,9},{11,1... | collective-permute-start | bytes 294920 | tf_op jit(solution)/shard_map/ppermute | solution.py:20
  46.6 1.0 copy-start.7
  46.7 1.0 copy-start.8
  46.7 1.0 copy-start.4
  46.7 1.0 copy-start.5
  48.2 1.0 copy-start.3
  49.1 0.9 copy-start.1
  167.9 26.5 %copy-start.6 = (bf16[3,3,3,128,4]{3,4,2,1,0:T(4,128)(2,1)S(1)}, bf16[3,3,3,128,4]{3,4,2,1,0:T(4,128)(2,1)}, u32[]{:S(2)}) copy-start(bf16[3,3,3,128,4]{3,4,2,1,0:T(4,128)(2,1)} %param.13) | copy-start | bytes 82948
  195.6 23.0 %all-to-all-start.4 = ((bf16[32,3,3,3,128,4]{4,5,3,2,1,0:T(4,128)(2,1)}), bf16[32,3,3,3,128,4]{4,5,3,2,1,0:T(4,128)(2,1)S(1)}, u32[]{:S(2)}, u32[]{:S(2)}) async-start(bf16[32,3,3,3,128,4]{4,5,3,2,1,0:T(4,128)(2,1)} %broadcast_in_dim.34), calls=%async_computation.4 | async-start | bytes 1769472 | tf_op jit(solution)/shard_map/all_to_all | solution.py:27
  220.1 101.5 %all-to-all-start.3 = ((f32[32,16,918]{2,1,0:T(8,128)}), f32[32,16,918]{2,1,0:T(8,128)S(1)}, u32[]{:S(2)}, u32[]{:S(2)}) async-start(f32[32,16,918]{2,1,0:T(8,128)} %broadcast_in_dim.33), calls=%async_computation.3 | async-start | bytes 4194304 | tf_op jit(solution)/shard_map/all_to_all | solution.py:27
  232.6 5.8 %copy-start.2 = (bf16[1,2,64,3456]{3,2,1,0:T(8,128)(2,1)S(1)}, bf16[1,2,64,3456]{3,2,1,0:T(8,128)(2,1)}, u32[]{:S(2)}) copy-start(bf16[1,2,64,3456]{3,2,1,0:T(8,128)(2,1)} %copy-done.1) | copy-start | bytes 2654212
  321.7 1.3 copy-start
  335.1 1.5 slice-start
where the time goes:
time: 346 us; the launch traced here: 340 us
  blocking collectives  138 us (40%)
  waiting for transfers between devices  97.1 us (28%)
  local copies, waits for them, and re-layouts  49 us (14%)
  starting transfers between devices  38 us (11%)
  matrix products  6.87 us (2%)
  other arithmetic  6.23 us (2%)
  loops' own time  4.09 us (1%)
    all_to_all x1, blocking collectives, sent_and_summed(): lax.all_to_all(pieces, axis, split_axis=0, concat_axis=0, tiled=True)  111 us
    all_to_all x2, waiting for transfers between devices, sent_to_all(): lax.all_to_all(jnp.broadcast_to(x[None], (peers, *x.shape)), axis, 0, 0,...  96.3 us
    all_to_all x1, blocking collectives, sum_by_axis(): return jnp.sum(lax.all_to_all(own, far, 0, 0, tiled=True), axis=0)  16.5 us
    all_to_all x2, starting transfers between devices, sent_to_all(): lax.all_to_all(jnp.broadcast_to(x[None], (peers, *x.shape)), axis, 0, 0,...  15.1 us
    ppermute x4, starting transfers between devices, padded_2(): after = lax.ppermute(leading, axis, down)  13.8 us
    slice x4, local copies, waits for them, and re-layouts, together(): running[b:e].reshape(a.shape)  10.8 us
    all_to_all x1, blocking collectives, sent_to_all(): lax.all_to_all(jnp.broadcast_to(x[None], (peers, *x.shape)), axis, 0, 0,...  9.75 us
    ppermute x4, starting transfers between devices, padded_2(): before = lax.ppermute(last, axis, up)  9.13 us
  transfers between devices with their start and end apart: 10, of which 3 were waited for; matrix products, arithmetic and copies ran while one was open for 9% of the time, Pallas kernels for 0%

commit v1 on v0

--- a/solution.py
+++ b/solution.py
@@ -176,7 +176,9 @@
     planes = padded.shape[0] - 2
     height = padded.shape[1] - 2
     breadth = padded.shape[2] - 2
-    full_weight = gather_directly(coarse_weight, DEPTH, 4)
+    turned = jnp.transpose(coarse_weight, (0, 1, 2, 4, 3))
+    turned = lax.all_gather(turned, DEPTH, axis=3, tiled=True)
+    full_weight = jnp.transpose(turned, (0, 1, 2, 4, 3))
     source = coarse_taps(padded, 0, channels, planes, height, breadth)
     upstream = coarse_taps(padded, channels, channels, planes, height, breadth)
     center = padded[1 : planes + 1, 1 : height + 1, 1 : breadth + 1, channels:].reshape(
@@ -194,14 +196,12 @@
     coarse_dx = coarse_dx.astype(jnp.bfloat16).reshape(planes, height, breadth, channels)
     shard_rows = channels // lax.axis_size(DEPTH)
     partial_value = lax.dot_general(
-        source, center, (((0,), (0,)), ((), ())), preferred_element_type=jnp.float32
-    )
-    middle_part, summed = together(
-        (middle_part, partial_value), (("depth_0", "depth_1"), ("depth_2", "height"))
-    )
-    anchor = lax.axis_index(DEPTH) * shard_rows
-    coarse_share = lax.dynamic_slice_in_dim(summed, anchor, shard_rows, 1)
-    coarse_dw = coarse_share.reshape(3, 3, 3, channels, shard_rows) * (
+        center, source, (((0,), (0,)), ((), ())), preferred_element_type=jnp.float32
+    )
+    coarse_share = lax.psum_scatter(partial_value, DEPTH, scatter_dimension=0, tiled=True)
+    coarse_share = lax.psum(coarse_share, "height")
+    middle_part = lax.psum(middle_part, DEPTH + ("height",))
+    coarse_dw = coarse_share.T.reshape(3, 3, 3, channels, shard_rows) * (
         1.0 / math.sqrt(coarse_cells)
     )
     middle_dw = middle_part * (1.0 / math.sqrt(middle_cells))

time: 346 us -> 808 us (2.34)
  waiting for transfers between devices: 97.1 us -> 570 us
  blocking collectives: 138 us -> 85.3 us
  local copies, waits for them, and re-layouts: 49 us -> 71.1 us
  between operations: 1.18 us -> 15.1 us
  starting transfers between devices: 38 us -> 27.5 us
    psum x0 -> x1, waiting for transfers between devices: none -> 434 us  [per_device(): middle_part = lax.psum(middle_part, DEPTH + ('height',))]
    all_to_all x3 -> x0, blocking collectives: 138 us -> none  [the longest x1 111 us: sent_and_summed(): lax.all_to_all(pieces, axis, split_axis=0, concat_axis=0, tiled=True)]
    unnamed x0 -> x3, waiting for transfers between devices: none -> 136 us
    all_to_all x2 -> x0, waiting for transfers between devices: 96.3 us -> none  [sent_to_all(): lax.all_to_all(jnp.broadcast_to(x[None], (peers, *x.shape)), axis, 0, 0,...]
    psum x0 -> x1, blocking collectives: none -> 61.2 us  [per_device(): coarse_share = lax.psum(coarse_share, 'height')]
    while x52, local copies, waits for them, and re-layouts: 6.63 us -> 37.2 us
    all_gather x0 -> x1, blocking collectives: none -> 24.1 us  [per_device(): turned = lax.all_gather(turned, DEPTH, axis=3, tiled=True)]
    all_to_all x2 -> x0, starting transfers between devices: 15.1 us -> none  [sent_to_all(): lax.all_to_all(jnp.broadcast_to(x[None], (peers, *x.shape)), axis, 0, 0,...]
  transfers between devices with their start and end apart: 10 -> 10, of which waited for: 3 -> 2; matrix products, arithmetic and copies ran while one was open for 9% -> 11% of each run, Pallas kernels for 0% -> 0%
where the time goes in v1:
time: 808 us; the launch traced here: 795 us
  waiting for transfers between devices  570 us (71%)
  blocking collectives  85.3 us (11%)
  local copies, waits for them, and re-layouts  71.1 us (9%)
  starting transfers between devices  27.5 us (3%)
  between operations  15.1 us (2%)
  matrix products  13.6 us (2%)
  other arithmetic  8.73 us (1%)
    psum x1, waiting for transfers between devices, per_device(): middle_part = lax.psum(middle_part, DEPTH + ('height',))  434 us
    unnamed x3, waiting for transfers between devices  136 us
    psum x1, blocking collectives, per_device(): coarse_share = lax.psum(coarse_share, 'height')  61.2 us
    while x52, local copies, waits for them, and re-layouts  37.2 us
    all_gather x1, blocking collectives, per_device(): turned = lax.all_gather(turned, DEPTH, axis=3, tiled=True)  24.1 us
    unnamed x44, local copies, waits for them, and re-layouts  19.6 us
  transfers between devices with their start and end apart: 10, of which 2 were waited for; matrix products, arithmetic and copies ran while one was open for 11% of the time, Pallas kernels for 0%

profile of v1, /device:TPU:1, one launch (start us, length us, event | category | flops | bytes accessed | tf_op | source)
XLA Modules:
  0.0 794.8 jit_solution(3421071362306720712)
XLA Ops:
  7.2 0.8 constant_dynamic-update-slice_fusion.59
  8.0 0.8 constant_dynamic-update-slice_fusion.58
  8.8 8.8 %collective-permute-start.5 = (bf16[1,2,64,256]{3,2,1,0:T(8,128)(2,1)S(1)}, bf16[1,2,64,256]{3,2,1,0:T(8,128)(2,1)S(1)}, u32[]{:S(2)}, u32[]{:S(2)}) collective-permute-start(bf16[1,2,64,256]{3,2,1,0:T(8,128)(2,1)S(1)} %constant_dynamic-update-slice_fusion.58), channel_id=1, source_target_pairs={{16,0},{32,16},{48,32},{64,48},{80,64},{96,80},{112,96},{128,112},... | collective-permute-start | bytes 196616 | tf_op jit(solution)/shard_map/ppermute | solution.py:20
  17.6 1.9 collective-permute-start.4
  19.5 0.9 constant_dynamic-update-slice_fusion.57
  20.4 0.9 constant_dynamic-update-slice_fusion.56
  21.3 2.4 collective-permute-start.1
  23.7 3.2 collective-permute-start
  26.9 1.7 copy.34
  28.6 0.8 copy.57
  29.4 24.1 %all_gather.3 = bf16[3,3,3,128,128]{4,2,1,0,3:T(4,128)(2,1)S(1)} all-gather(bf16[3,3,3,4,128]{4,2,1,0,3:T(4,128)(2,1)S(1)} %bitcast.97), channel_id=1, replica_groups=mesh['depth_0'=4,'depth_1'=4,'depth_2'=2,'height'=16] {'depth_0','depth_..., dimensions={3}, use_global_device_ids=true | all-gather | bytes 912384 | tf_op jit(solution)/shard_map/all_gather | solution.py:180
  53.6 0.8 reshape.60
  54.4 1.0 copy.31
  56.0 1.3 collective-permute-start.3
  57.3 4.2 collective-permute-start.2
  61.5 1.3 collective-permute-start.7
  62.8 4.2 collective-permute-start.6
  67.0 2.6 select_maximum_fusion
  69.7 54.0 %while.15 = (s32[]{:T(128)}, f32[864,32]{0,1:T(8,128)S(1)}, bf16[2,32,4,128]{3,2,1,0:T(4,128)(2,1)S(1)}, bf16[2,32,4,128]{3,2,1,0:T(4,128)(2,1)}, s32[2]{0:T(128...) while((s32[]{:T(128)}, f32[864,32]{0,1:T(8,128)S(1)}, ...), condition=%wide.region_1.2_spmd.clone, body=%wide.region_0.1_spmd.clone.sunk | while | flops 85022728 | bytes 6918741 | solution.py:148
  75.8 0.8 constant_dynamic-update-slice_fusion.147
  81.5 0.8 constant_dynamic-update-slice_fusion.155
  82.2 0.8 constant_dynamic-update-slice_fusion.156
  87.9 0.8 constant_dynamic-update-slice_fusion.164
  90.1 0.8 constant_dynamic-update-slice_fusion.167
  91.6 1.5 convolution_add_fusion.2
  93.2 1.4 fusion.47
  94.6 1.4 fusion.48
  105.0 0.8 constant_dynamic-update-slice_fusion.150
  108.5 0.8 constant_dynamic-update-slice_fusion.155
  109.3 0.8 constant_dynamic-update-slice_fusion.156
  114.9 0.8 constant_dynamic-update-slice_fusion.164
  117.1 0.8 constant_dynamic-update-slice_fusion.167
  118.6 1.5 convolution_add_fusion.2
  120.2 1.4 fusion.47
  121.6 1.4 fusion.48
  123.8 1.0 copy.29
  142.3 1.7 convolution_bitcast_fusion
  144.0 1.0 reverse_bitcast_fusion
  145.0 2.0 copy.32
  147.0 1.3 dynamic-slice
  148.9 1.0 convolution_convert_fusion.3
  149.9 2.2 convolution_convert_fusion.2
  152.1 433.7 %all-reduce.6.cloned.1.call-done = f32[3,3,3,32,32]{4,3,2,1,0:T(8,128)} async-done(((f32[3,3,3,32,32]{4,3,2,1,0:T(8,128)}), f32[3,3,3,32,32]{4,3,2,1,0:T(8,128)}) %all-reduce.6.cloned.1.call-update) | async-done | bytes 110608 | tf_op jit(solution)/shard_map/psum | solution.py:203
  585.8 1.8 broadcast_multiply_fusion.1
  587.6 135.8 %all-reduce.8.cloned.1.call-done = f32[128,3456]{0,1:T(8,128)} async-done(((f32[128,3456]{0,1:T(8,128)}), f32[128,3456]{0,1:T(8,128)}) %all-reduce.8.cloned.1.call-update) | async-done | bytes 1769488
  723.4 2.0 constant_dynamic-slice_fusion
  725.4 61.2 %psum.15 = f32[4,3456]{0,1:T(8,128)S(1)} all-reduce(f32[4,3456]{0,1:T(8,128)S(1)} %constant_dynamic-slice_fusion), channel_id=1, replica_groups=mesh['depth_0'=4,'depth_1'=4,'depth_2'=2,'height'=16] {'height'}, use_global_device_ids=true, to_apply=%region_4.5 | all-reduce | flops 13824 | bytes 110592 | tf_op jit(solution)/shard_map/psum | solution.py:202
  786.8 1.2 copy.33
  (122 shorter events, 52.1 us)
Async XLA Ops:
  7.2 46.3 %copy-start = (bf16[3,3,3,32,32]{4,3,2,1,0:T(8,128)(2,1)S(1)}, bf16[3,3,3,32,32]{4,3,2,1,0:T(8,128)(2,1)}, u32[]{:S(2)}) copy-start(bf16[3,3,3,32,32]{4,3,2,1,0:T(8,128)(2,1)} %param.10) | copy-start | bytes 165892
  7.2 578.6 %all-reduce.6.cloned.1.call-start = ((), (), s32[]{:S(2)}) async-start(), calls=%async_computation | async-start | bytes 884736 | tf_op jit(solution)/shard_map/psum | solution.py:203
  8.8 52.6 %collective-permute-start.5 = (bf16[1,2,64,256]{3,2,1,0:T(8,128)(2,1)S(1)}, bf16[1,2,64,256]{3,2,1,0:T(8,128)(2,1)S(1)}, u32[]{:S(2)}, u32[]{:S(2)}) collective-permute-start(bf16[1,2,64,256]{3,2,1,0:T(8,128)(2,1)S(1)} %constant_dynamic-update-slice_fusion.58), channel_id=1, source_target_pairs={{16,0},{32,16},{48,32},{64,48},{80,64},{96,80},{112,96},{128,112},... | collective-permute-start | bytes 196616 | tf_op jit(solution)/shard_map/ppermute | solution.py:20
  17.6 43.9 %collective-permute-start.4 = (bf16[1,2,64,256]{3,2,1,0:T(8,128)(2,1)S(1)}, bf16[1,2,64,256]{3,2,1,0:T(8,128)(2,1)S(1)}, u32[]{:S(2)}, u32[]{:S(2)}) collective-permute-start(bf16[1,2,64,256]{3,2,1,0:T(8,128)(2,1)S(1)} %constant_dynamic-update-slice_fusion.58), channel_id=1, source_target_pairs={{0,16},{16,32},{32,48},{48,64},{64,80},{80,96},{96,112},{112,128},... | collective-permute-start | bytes 196616 | tf_op jit(solution)/shard_map/ppermute | solution.py:19
  21.3 34.2 %collective-permute-start.1 = (bf16[1,64,4,128]{3,2,1,0:T(4,128)(2,1)S(1)}, bf16[1,64,4,128]{3,2,1,0:T(4,128)(2,1)S(1)}, u32[]{:S(2)}, u32[]{:S(2)}) collective-permute-start(bf16[1,64,4,128]{3,2,1,0:T(4,128)(2,1)S(1)} %get-tuple-element.230), channel_id=1, source_target_pairs={{16,0},{32,16},{48,32},{64,48},{80,64},{96,80},{112,96},{128,112},... | collective-permute-start | bytes 196616 | tf_op jit(solution)/shard_map/ppermute | solution.py:20
  23.7 31.8 %collective-permute-start = (bf16[1,64,4,128]{3,2,1,0:T(4,128)(2,1)S(1)}, bf16[1,64,4,128]{3,2,1,0:T(4,128)(2,1)S(1)}, u32[]{:S(2)}, u32[]{:S(2)}) collective-permute-start(bf16[1,64,4,128]{3,2,1,0:T(4,128)(2,1)S(1)} %get-tuple-element.229), channel_id=1, source_target_pairs={{0,16},{16,32},{32,48},{48,64},{64,80},{80,96},{96,112},{112,128},... | collective-permute-start | bytes 196616 | tf_op jit(solution)/shard_map/ppermute | solution.py:19
  55.5 14.2 %copy-start.4 = (f32[864,32]{0,1:T(8,128)S(1)}, f32[864,32]{0,1:T(8,128)}, u32[]{:S(2)}) copy-start(f32[864,32]{0,1:T(8,128)} %custom-call) | copy-start | bytes 331780
  55.5 14.2 %copy-start.5 = (bf16[864,32]{0,1:T(8,128)(2,1)S(1)}, bf16[864,32]{0,1:T(8,128)(2,1)}, u32[]{:S(2)}) copy-start(bf16[864,32]{0,1:T(8,128)(2,1)} %copy.34) | copy-start | bytes 165892
  55.5 14.2 %copy-start.6 = (bf16[864,32]{0,1:T(8,128)(2,1)S(1)}, bf16[864,32]{0,1:T(8,128)(2,1)}, u32[]{:S(2)}) copy-start(bf16[864,32]{0,1:T(8,128)(2,1)} %reshape.60) | copy-start | bytes 165892
  55.5 14.2 %copy-start.7 = (bf16[2,32,4,128]{3,2,1,0:T(4,128)(2,1)S(1)}, bf16[2,32,4,128]{3,2,1,0:T(4,128)(2,1)}, u32[]{:S(2)}) copy-start(bf16[2,32,4,128]{3,2,1,0:T(4,128)(2,1)} %custom-call.7) | copy-start | bytes 196612
  55.5 11.5 %copy-start.2 = (bf16[1,64,4,128]{3,2,1,0:T(4,128)(2,1)}, bf16[1,64,4,128]{3,2,1,0:T(4,128)(2,1)S(1)}, u32[]{:S(2)}) copy-start(bf16[1,64,4,128]{3,2,1,0:T(4,128)(2,1)S(1)} %collective-permute-done) | copy-start | bytes 196612
  56.0 11.0 %collective-permute-start.3 = (bf16[4,64,1,128]{3,2,1,0:T(2,128)(2,1)S(1)}, bf16[4,64,1,128]{3,2,1,0:T(2,128)(2,1)S(1)}, u32[]{:S(2)}, u32[]{:S(2)}) collective-permute-start(bf16[4,64,1,128]{3,2,1,0:T(2,128)(2,1)S(1)} %get-tuple-element.226), channel_id=1, source_target_pairs={{1,0},{2,1},{3,2},{4,3},{5,4},{6,5},{7,6},{8,7},{9,8},{10,9},{11,1... | collective-permute-start | bytes 196616 | tf_op jit(solution)/shard_map/ppermute | solution.py:20
  57.3 9.8 %collective-permute-start.2 = (bf16[4,64,1,128]{3,2,1,0:T(2,128)(2,1)S(1)}, bf16[4,64,1,128]{3,2,1,0:T(2,128)(2,1)S(1)}, u32[]{:S(2)}, u32[]{:S(2)}) collective-permute-start(bf16[4,64,1,128]{3,2,1,0:T(2,128)(2,1)S(1)} %get-tuple-element.225), channel_id=1, source_target_pairs={{0,1},{1,2},{2,3},{3,4},{4,5},{5,6},{6,7},{7,8},{8,9},{9,10},{10,1... | collective-permute-start | bytes 196616 | tf_op jit(solution)/shard_map/ppermute | solution.py:19
  61.5 63.5 %collective-permute-start.7 = (bf16[3,1,64,256]{3,2,1,0:T(8,128)(2,1)S(1)}, bf16[3,1,64,256]{3,2,1,0:T(8,128)(2,1)S(1)}, u32[]{:S(2)}, u32[]{:S(2)}) collective-permute-start(bf16[3,1,64,256]{3,2,1,0:T(8,128)(2,1)S(1)} %get-tuple-element.228), channel_id=1, source_target_pairs={{1,0},{2,1},{3,2},{4,3},{5,4},{6,5},{7,6},{8,7},{9,8},{10,9},{11,1... | collective-permute-start | bytes 294920 | tf_op jit(solution)/shard_map/ppermute | solution.py:20
  62.8 62.2 %collective-permute-start.6 = (bf16[3,1,64,256]{3,2,1,0:T(8,128)(2,1)S(1)}, bf16[3,1,64,256]{3,2,1,0:T(8,128)(2,1)S(1)}, u32[]{:S(2)}, u32[]{:S(2)}) collective-permute-start(bf16[3,1,64,256]{3,2,1,0:T(8,128)(2,1)S(1)} %get-tuple-element.227), channel_id=1, source_target_pairs={{0,1},{1,2},{2,3},{3,4},{4,5},{5,6},{6,7},{7,8},{8,9},{9,10},{10,1... | collective-permute-start | bytes 294920 | tf_op jit(solution)/shard_map/ppermute | solution.py:19
  123.8 7.7 copy-start.8
  124.7 8.6 %copy-start.1 = (bf16[1,2,64,128]{3,2,1,0:T(8,128)(2,1)S(1)}, bf16[1,2,64,128]{3,2,1,0:T(8,128)(2,1)}, u32[]{:S(2)}) copy-start(bf16[1,2,64,128]{3,2,1,0:T(8,128)(2,1)} %param.12) | copy-start | bytes 98308
  124.7 8.6 %copy-start.3 = (bf16[1,2,64,128]{3,2,1,0:T(8,128)(2,1)S(1)}, bf16[1,2,64,128]{3,2,1,0:T(8,128)(2,1)}, u32[]{:S(2)}) copy-start(bf16[1,2,64,128]{3,2,1,0:T(8,128)(2,1)} %param.11) | copy-start | bytes 98308
  124.7 598.7 %all-reduce.8.cloned.1.call-start = ((), (), s32[]{:S(2)}) async-start(), calls=%async_computation.1 | async-start | bytes 3538944
Sparse Core Ops, SparseCore 0:
  124.9 460.8 all-reduce.5
  589.5 133.8 all-reduce.7

commit v2 on v1

v2 whole, which is shorter than its diff:
```python
import functools
import math

import jax
import jax.numpy as jnp
from jax import lax
from jax.experimental import pallas as pl
from jax.experimental.pallas import tpu as pltpu
from jax.sharding import PartitionSpec as P

MESH = pl.DeviceIdType.MESH
F32 = jnp.float32
BF16 = jnp.bfloat16
NT = (((1,), (1,)), ((), ()))
NN = (((1,), (0,)), ((), ()))


def dot(a, b, dims):
    return lax.dot_general(a, b, dims, preferred_element_type=F32)


def kernel(
    D,
    Z,
    middle_scale,
    coarse_scale,
    m_ref,
    wf_ref,
    wb_ref,
    xc_ref,
    gc_ref,
    gt_ref,
    ws_ref,
    mo_ref,
    mdx_ref,
    mw_ref,
    co_ref,
    cdx_ref,
    cw_ref,
    me,
    mv,
    mr,
    mrl,
    own,
    xg,
    wg,
    ggl,
    gg,
    tf,
    hr,
    gd,
    xcol,
    gcol,
    zl,
    mg,
    loc,
    ga_s,
    ga_r,
    x_s,
    x_r,
    gb_s,
    gb_r,
    w_s,
    w_r,
    ch_s,
    ch_r,
    mh_s,
    mh_r,
    mr_s,
    mr_r,
    mg_s,
    mg_r,
    ring_s,
    ring_r,
):
    d = lax.axis_index("depth")
    z = lax.axis_index("height")
    CO = 128 // D
    RB = tf.shape[1]
    n = 32 // D
    up = lax.rem(z + 1, Z)
    down = lax.rem(z + Z - 1, Z)
    after = lax.rem(d + 1, D)
    before = lax.rem(d + D - 1, D)

    barrier = pltpu.get_barrier_semaphore()

    def greet(k, carry):
        pl.semaphore_signal(
            barrier, inc=1, device_id=(lax.rem(d + k, D), z), device_id_type=MESH
        )
        return carry

    for zz in (up, down):
        for dd in (before, d, after):
            pl.semaphore_signal(barrier, inc=1, device_id=(dd, zz), device_id_type=MESH)
    lax.fori_loop(1, D, greet, 0)
    pl.semaphore_wait(barrier, D - 1 + 6)

    def remote(src, dst, s, r, to):
        return pltpu.make_async_remote_copy(
            src_ref=src, dst_ref=dst, send_sem=s, recv_sem=r, device_id=to, device_id_type=MESH
        )

    local = [
        pltpu.make_async_copy(gt_ref, ggl.at[:, 1], loc.at[0]),
        pltpu.make_async_copy(xc_ref, xg.at[d], loc.at[1]),
        pltpu.make_async_copy(ws_ref, wg.at[d], loc.at[2]),
        pltpu.make_async_copy(m_ref, me.at[1:3, 1:5], loc.at[3]),
    ]
    for c in local:
        c.start()

    ga = [
        remote(gt_ref, ggl.at[:, 0], ga_s.at[0], ga_r.at[0], (d, up)),
        remote(gt_ref, ggl.at[:, 2], ga_s.at[1], ga_r.at[1], (d, down)),
    ]
    for c in ga:
        c.start()

    mh = []
    for i, (dst, src, to) in enumerate(
        (
            (me.at[0, 1:5], m_ref.at[1], (after, z)),
            (me.at[3, 1:5], m_ref.at[0], (before, z)),
            (me.at[1:3, 0], m_ref.at[:, 3], (d, up)),
            (me.at[1:3, 5], m_ref.at[:, 0], (d, down)),
            (me.at[0, 0], m_ref.at[1, 3], (after, up)),
            (me.at[0, 5], m_ref.at[1, 0], (after, down)),
            (me.at[3, 0], m_ref.at[0, 3], (before, up)),
            (me.at[3, 5], m_ref.at[0, 0], (before, down)),
        )
    ):
        mh.append(remote(src, dst, mh_s.at[i], mh_r.at[i], to))
    for c in mh:
        c.start()

    def to_plane(src, dst, s, r):
        def one(k, carry):
            e = lax.rem(d + k, D)
            remote(src(e), dst, s, r, (e, z)).start()
            return carry

        lax.fori_loop(1, D, one, 0)

    def from_plane(whole, s, r, both=True):
        rest = whole.at[pl.ds(0, D - 1)]
        c = remote(rest, rest, s, r, (after, z))
        c.wait_recv()
        c.wait_send()

    to_plane(lambda e: xc_ref, xg.at[d], x_s, x_r)

    ch = []
    for ai, to_d in ((0, after), (1, d), (2, before)):
        for ud, to_z in ((0, up), (1, down)):
            for k, ref in ((0, xc_ref), (1, gc_ref)):
                i = (ai * 2 + ud) * 2 + k
                ch.append(
                    remote(
                        ref.at[pl.ds(64 * (1 - ud), 64)],
                        hr.at[ai, ud, k],
                        ch_s.at[i],
                        ch_r.at[i],
                        (to_d, to_z),
                    )
                )
    ch.append(remote(gc_ref, gd.at[0], ch_s.at[12], ch_r.at[12], (after, z)))
    ch.append(remote(gc_ref, gd.at[1], ch_s.at[13], ch_r.at[13], (before, z)))
    for c in ch:
        c.start()

    local[0].wait()
    for c in ga:
        c.wait()
    keep = pltpu.make_async_copy(ggl.at[d], gg.at[d], loc.at[4])
    keep.start()
    to_plane(lambda e: ggl.at[e], gg.at[d], gb_s, gb_r)
    to_plane(lambda e: ws_ref, wg.at[d], w_s, w_r)

    local[3].wait()
    for c in mh:
        c.wait()
    depth_ok = (d > 0, None, None, d < D - 1)
    height_ok = (z > 0, None, None, None, None, z < Z - 1)
    lane = lax.broadcasted_iota(jnp.int32, (64, 128), 1)
    for dd in range(4):
        for hh in range(6):
            row = me[dd, hh].astype(F32)
            for ok in (depth_ok[dd], height_ok[hh]):
                if ok is not None:
                    row = jnp.where(ok, row, 0.0)
            left = jnp.where(lane == 0, 0.0, pltpu.roll(row, 1, 1))
            right = jnp.where(lane == 127, 0.0, pltpu.roll(row, 127, 1))
            for c, v in enumerate((left, row, right)):
                v = v.astype(BF16)
                mv[dd, hh, 0, 32 * c : 32 * c + 32] = v[:32]
                mv[dd, hh, 1, 32 * c : 32 * c + 32] = v[32:]

    def columns(dd, k):
        return jnp.concatenate(
            [
                jnp.concatenate([mv[dd, h + b, k] for h in range(4)], axis=1)
                for b in range(3)
            ],
            axis=0,
        )

    seen = [
        jnp.concatenate([mv[dd + 1, h + 1, 1, 32:64] for h in range(4)], axis=1)
        for dd in range(2)
    ]
    grad = [None] * 3
    outs = [None] * 2
    for dd in range(4):
        cols = columns(dd, 0)
        part = dot(wf_ref[...], cols, NN)
        for a in range(3):
            at = dd - a
            if 0 <= at < 2:
                p = part[32 * a : 32 * a + 32]
                outs[at] = p if outs[at] is None else outs[at] + p
                g = dot(seen[at], cols, NT)
                grad[a] = g if grad[a] is None else grad[a] + g
    flat = jnp.concatenate(grad + [jnp.zeros((32, 32), F32)], axis=1)
    for ob in range(4):
        for j in range(7):
            mr[ob * 7 + j] = flat[8 * ob : 8 * ob + 8, 128 * j : 128 * j + 128]
    for t in range(28, 32):
        mr[t] = jnp.zeros((8, 128), F32)
    keep_mr = pltpu.make_async_copy(mr.at[pl.ds(d * n, n)], mrl.at[d], loc.at[5])
    keep_mr.start()
    to_plane(lambda e: mr.at[pl.ds(e * n, n)], mrl.at[d], mr_s, mr_r)
    for at in range(2):
        for h in range(4):
            mo_ref[at, h] = outs[at][:, 128 * h : 128 * h + 128].astype(BF16)
    outs = [None] * 2
    for dd in range(4):
        part = dot(wb_ref[...], columns(dd, 1), NN)
        for a in range(3):
            at = dd - a
            if 0 <= at < 2:
                p = part[32 * a : 32 * a + 32]
                outs[at] = p if outs[at] is None else outs[at] + p
    for at in range(2):
        for h in range(4):
            mdx_ref[at, h] = outs[at][:, 128 * h : 128 * h + 128].astype(BF16)

    tf[...] = jnp.zeros(tf.shape, F32)
    keep.wait()
    from_plane(gg, gb_s, gb_r)
    lanes = lax.broadcasted_iota(jnp.int32, (D, CO, 128), 2)
    first = lanes < 64
    below = jnp.where(z > 0, gg[:, 0], 0.0)
    here = gg[:, 1]
    above = jnp.where(z < Z - 1, gg[:, 2], 0.0)

    def turned(v, amount):
        return pltpu.roll(v.reshape(D * CO, 128), amount, 1).reshape(D, CO, 128)

    here_half = turned(here, 64)
    bases = (
        jnp.where(first, here_half, turned(above, 64)),
        here,
        jnp.where(first, turned(below, 64), here_half),
    )
    column = lanes % 64
    for b in range(3):
        base = bases[b]
        shifted = (
            jnp.where(column == 63, 0.0, turned(base, 127)),
            base,
            jnp.where(column == 0, 0.0, turned(base, 1)),
        )
        for c in range(3):
            at = (b * 3 + c) * CO
            tf[1 : D + 1, at : at + CO, :] = shifted[c]
    local[1].wait()
    from_plane(xg, x_s, x_r)

    def plane_pair(k, acc):
        s = 2 * k
        taps = jnp.concatenate(
            [
                tf[pl.ds(s, 3)].reshape(3 * RB, 128).astype(BF16),
                tf[pl.ds(s + 1, 3)].reshape(3 * RB, 128).astype(BF16),
            ],
            axis=1,
        )
        return acc + dot(taps, xg[pl.ds(s, 2)].reshape(256, 128), NN)

    acc = lax.fori_loop(0, D // 2, plane_pair, jnp.zeros((3 * RB, 128), F32))
    for a in range(3):
        zl[z, a * RB : (a + 1) * RB, :] = acc[(2 - a) * RB : (3 - a) * RB]
    keep_mr.wait()
    from_plane(mrl, mr_s, mr_r)
    total = mrl[0]
    for e in range(1, D):
        total = total + mrl[e]
    zl[z, 3 * RB : 3 * RB + 8 * n, :] = total.reshape(8 * n, 128)

    far = Z // 2

    def hop(way, step):
        if way == 0:
            slot = zl.at[lax.rem(z + Z - step, Z)]
            to = up
        else:
            slot = zl.at[lax.rem(z + step, Z)]
            to = down
        return remote(slot, slot, ring_s.at[way, step], ring_r.at[way, step], (d, to))

    def serve(step):
        if step > 0:
            hop(0, step - 1).wait()
            if step - 1 < far - 1:
                hop(1, step - 1).wait()
        if step < far:
            hop(0, step).start()
        if step < far - 1:
            hop(1, step).start()

    serve(0)

    for c in ch:
        c.wait()
    row_ok = (z > 0, None, z < Z - 1)
    place = lax.broadcasted_iota(jnp.int32, (256, 128), 0) % 64
    for a in range(3):
        near = jnp.clip(d + a - 1, 0, D - 1)
        for k, col in ((0, xcol), (1, gcol)):
            if k == 0:
                centre = xg[near]
            else:
                centre = gc_ref[...] if a == 1 else gd[a // 2]
            low = jnp.where(z > 0, hr[a, 0, k].astype(F32), 0.0)
            high = jnp.where(z < Z - 1, hr[a, 1, k].astype(F32), 0.0)
            rows = jnp.concatenate([low, centre.astype(F32), high], axis=0)
            if a == 0:
                rows = jnp.where(d > 0, rows, 0.0)
            if a == 2:
                rows = jnp.where(d < D - 1, rows, 0.0)
            prev = jnp.where(place == 0, 0.0, pltpu.roll(rows, 1, 0))
            nxt = jnp.where(place == 63, 0.0, pltpu.roll(rows, 255, 0))
            for c, v in enumerate((prev, rows, nxt)):
                col[a, :, 128 * c : 128 * c + 128] = v.astype(BF16)
    serve(1)
    local[2].wait()
    from_plane(wg, w_s, w_r)

    def tap(t):
        w = wg[:, t].astype(F32)
        if CO % 8:
            w = w.reshape(D // 2, 2, CO, 128)
            w = jnp.concatenate([w[:, 0], w[:, 1]], axis=1)
        return w.reshape(128, 128).astype(BF16)

    out = jnp.zeros((128, 128), F32)
    dx = jnp.zeros((128, 128), F32)
    step = 2
    for a in range(3):
        for b in range(3):
            w = [tap((a * 3 + b) * 3 + c) for c in range(3)]
            out = out + dot(xcol[a, 64 * b : 64 * b + 128, :], jnp.concatenate(w, axis=1), NT)
            dx = dx + dot(
                gcol[2 - a, 64 * (2 - b) : 64 * (2 - b) + 128, :],
                jnp.concatenate(w[::-1], axis=0),
                NN,
            )
            if step <= far:
                serve(step)
                step += 1
    co_ref[...] = out.astype(BF16)
    cdx_ref[...] = dx.astype(BF16)
    while step <= far:
        serve(step)
        step += 1

    total = zl[0]
    for s in range(1, Z):
        total = total + zl[s]
    cw_ref[...] = (total[: 3 * RB] * coarse_scale).reshape(3, RB, 128)
    own[...] = (total[3 * RB : 3 * RB + 8 * n] * middle_scale).reshape(n, 8, 128)
    keep_mg = pltpu.make_async_copy(own, mg.at[d], loc.at[6])
    keep_mg.start()
    to_plane(lambda e: own, mg.at[d], mg_s, mg_r)
    keep_mg.wait()
    from_plane(mg, mg_s, mg_r)
    mw_ref[...] = mg[...]


def per_device(D, Z, middle_input, middle_cotangent, middle_weight, coarse_input, coarse_cotangent, coarse_weight):
    CO = 128 // D
    RB = -(-9 * CO // 8) * 8
    n = 32 // D
    R = 3 * RB + 8 * n
    far = Z // 2
    middle_cells = middle_input.shape[0] * D * middle_input.shape[2] * Z * middle_input.shape[3]
    coarse_cells = coarse_input.shape[0] * D * coarse_input.shape[1] * Z * coarse_input.shape[2]
    m = jnp.concatenate(
        [jnp.swapaxes(middle_input, 1, 2), jnp.swapaxes(middle_cotangent, 1, 2)], axis=2
    )
    wf = jnp.transpose(middle_weight, (0, 4, 1, 2, 3)).reshape(96, 288)
    wb = jnp.transpose(middle_weight[::-1, ::-1, ::-1], (0, 3, 1, 2, 4)).reshape(96, 288)
    xc = coarse_input.reshape(128, 128)
    gc = coarse_cotangent.reshape(128, 128)
    gt = gc.T.astype(F32).reshape(D, CO, 128)
    ws = jnp.swapaxes(coarse_weight, 3, 4).reshape(27, CO, 128)
    dma = pltpu.SemaphoreType.DMA
    vmem = pl.BlockSpec(memory_space=pltpu.VMEM)
    mo, mdx, mw, co, cdx, cw = pl.pallas_call(
        functools.partial(
            kernel, D, Z, 1.0 / math.sqrt(middle_cells), 1.0 / math.sqrt(coarse_cells)
        ),
        out_shape=(
            jax.ShapeDtypeStruct((2, 4, 32, 128), BF16),
            jax.ShapeDtypeStruct((2, 4, 32, 128), BF16),
            jax.ShapeDtypeStruct((D, n, 8, 128), F32),
            jax.ShapeDtypeStruct((128, 128), BF16),
            jax.ShapeDtypeStruct((128, 128), BF16),
            jax.ShapeDtypeStruct((3, RB, 128), F32),
        ),
        in_specs=[vmem] * 7,
        out_specs=(vmem,) * 6,
        scratch_shapes=[
            pltpu.VMEM((4, 6, 64, 128), BF16),
            pltpu.VMEM((4, 6, 2, 96, 128), BF16),
            pltpu.VMEM((32, 8, 128), F32),
            pltpu.VMEM((D, n, 8, 128), F32),
            pltpu.VMEM((n, 8, 128), F32),
            pltpu.VMEM((D, 128, 128), BF16),
            pltpu.VMEM((D, 27, CO, 128), BF16),
            pltpu.VMEM((D, 3, CO, 128), F32),
            pltpu.VMEM((D, 3, CO, 128), F32),
            pltpu.VMEM((D + 2, RB, 128), F32),
            pltpu.VMEM((3, 2, 2, 64, 128), BF16),
            pltpu.VMEM((2, 128, 128), BF16),
            pltpu.VMEM((3, 256, 384), BF16),
            pltpu.VMEM((3, 256, 384), BF16),
            pltpu.VMEM((Z, R, 128), F32),
            pltpu.VMEM((D, n, 8, 128), F32),
            dma((7,)),
            dma((2,)),
            dma((2,)),
            dma,
            dma,
            dma,
            dma,
            dma,
            dma,
            dma((14,)),
            dma((14,)),
            dma((8,)),
            dma((8,)),
            dma,
            dma,
            dma,
            dma,
            dma((2, far)),
            dma((2, far)),
        ],
        compiler_params=pltpu.CompilerParams(collective_id=0, has_side_effects=True),
    )(m, wf, wb, xc, gc, gt, ws)
    middle_out = jnp.swapaxes(mo, 1, 2)
    middle_dx = jnp.swapaxes(mdx, 1, 2)
    tiles = mw.reshape(32, 8, 128)[:28].reshape(4, 7, 8, 128)
    flat = jnp.transpose(tiles, (0, 2, 1, 3)).reshape(32, 896)[:, :864]
    middle_dw = flat.T.reshape(3, 3, 3, 32, 32)
    coarse_dw = jnp.swapaxes(cw[:, : 9 * CO].reshape(3, 3, 3, CO, 128), 3, 4)
    return (
        middle_out,
        middle_dx,
        middle_dw,
        co.reshape(coarse_input.shape),
        cdx.reshape(coarse_input.shape),
        coarse_dw,
    )


def solution(mesh):
    placed = (
        P("depth", None, "height", None),
        P("depth", None, "height", None),
        P(),
        P("depth", "height", None, None),
        P("depth", "height", None, None),
        P(None, None, None, None, "depth"),
    )
    return jax.shard_map(
        functools.partial(per_device, mesh.shape["depth"], mesh.shape["height"]),
        mesh=mesh,
        in_specs=placed,
        out_specs=(
            placed[0],
            placed[1],
            P(),
            placed[3],
            placed[4],
            placed[5],
        ),
        check_vma=False,
    )
```

time: 808 us -> 102 us (0.13); the launches traced: 795 us -> 102 us
  waiting for transfers between devices: 570 us -> 0 us
  Pallas kernels: 0 us -> 91.3 us
  blocking collectives: 85.3 us -> 0 us
  local copies, waits for them, and re-layouts: 71.1 us -> 8.38 us
  starting transfers between devices: 27.5 us -> 0 us
  between operations: 15.1 us -> 0.71 us
  matrix products: 13.6 us -> 0 us
    psum x1 -> x0, waiting for transfers between devices: 434 us -> none  [per_device(): middle_part = lax.psum(middle_part, DEPTH + ('height',))]
    unnamed x3 -> x0, waiting for transfers between devices: 136 us -> none
    pallas_call x0 -> x1, Pallas kernels: none -> 91.3 us  [per_device(): pl.pallas_call(functools.partial(kernel, D, Z, 1.0 / math.sqrt(middle_cel...]
    psum x1 -> x0, blocking collectives: 61.2 us -> none  [per_device(): coarse_share = lax.psum(coarse_share, 'height')]
    while x53 -> x0, local copies, waits for them, and re-layouts: 38.1 us -> none
    ppermute x8 -> x0, starting transfers between devices: 27.2 us -> none  [the longest x4 13.8 us: padded_2(): after = lax.ppermute(leading, axis, down)]
    all_gather x1 -> x0, blocking collectives: 24.1 us -> none  [per_device(): turned = lax.all_gather(turned, DEPTH, axis=3, tiled=True)]
    unnamed x44 -> x21, local copies, waits for them, and re-layouts: 19.6 us -> 4.98 us
  transfers between devices with their start and end apart: 10 -> 0, of which waited for: 2 -> 0; matrix products, arithmetic and copies ran while one was open for 11% -> 0% of each run, Pallas kernels for 0% -> 0%
where the time goes in v2:
time: 102 us
  Pallas kernels  91.3 us (90%)
  local copies, waits for them, and re-layouts  8.38 us (8%)
  other arithmetic  1.43 us (1%)
    pallas_call x1, Pallas kernels, per_device(): pl.pallas_call(functools.partial(kernel, D, Z, 1.0 / math.sqrt(middle_cel...  91.3 us
    unnamed x21, local copies, waits for them, and re-layouts  4.98 us

profile of v2, /device:TPU:1, one launch (start us, length us, event | category | flops | bytes accessed | tf_op | source)
XLA Modules:
  0.0 101.8 jit_solution(12829337504045280629)
XLA Ops:
  0.6 0.8 convert_bitcast_fusion
  1.4 0.0 copy-start.3
  1.4 0.0 copy-start.4
  1.4 0.7 copy.31
  2.1 0.1 copy-done.3
  2.2 0.0 copy-done.4
  2.3 0.0 copy-start
  2.3 0.7 pad_maximum_fusion.m_ref
  3.0 0.3 copy-done
  3.3 0.2 copy.30
  3.4 0.8 reshape.54.wb_ref
  4.2 0.2 copy.29
  4.4 0.8 reshape.53.wf_ref
  5.3 91.3 %shard_map.109 = (bf16[2,4,32,128]{3,2,1,0:T(8,128)(2,1)}, bf16[2,4,32,128]{3,2,1,0:T(8,128)(2,1)}, f32[32,1,8,128]{3,2,1,0:T(8,128)}, bf16[128,128]{1,0:T(8,128...) custom-call(bf16[2,4,64,128]{3,2,1,0:T(8,128)(2,1)} %pad_maximum_fusion.m_ref, bf16[96,288]{1,0:T(8,128)(2,1)} %reshape.53.wf_ref, ...), custom_call_target="tpu_custom_call" | custom-call | tf_op jit(solution)/shard_map/pallas_call | solution.py:411
  96.6 0.0 copy-start.2
  96.6 0.0 copy-start.5
  96.6 1.5 %copy.32 = bf16[2,32,4,128]{3,2,1,0:T(4,128)(2,1)} copy(bf16[2,32,4,128]{3,1,2,0:T(8,128)(2,1)} %bitcast.36) | data formatting | bytes 131072
  98.1 0.0 copy-start.1
  98.1 0.0 copy-done.2
  98.1 0.7 copy.33
  98.8 0.0 copy-done.5
  98.8 0.6 reshape.65
  99.5 0.0 copy-done.1
  99.5 0.0 copy-start.7
  99.5 1.0 copy.35
  100.5 0.0 copy-done.7
  100.5 0.0 copy-start.6
  100.5 0.6 copy.40
  101.1 0.2 copy-done.6
  101.2 0.6 copy.41
  (4 shorter events, 0.1 us)
Async XLA Ops:
  1.4 0.8 copy-start.3
  1.4 0.9 copy-start.4
  2.3 1.0 copy-start
  96.6 1.6 %copy-start.2 = (bf16[2,4,32,128]{3,2,1,0:T(8,128)(2,1)S(1)}, bf16[2,4,32,128]{3,2,1,0:T(8,128)(2,1)}, u32[]{:S(2)}) copy-start(bf16[2,4,32,128]{3,2,1,0:T(8,128)(2,1)} %get-tuple-element.13) | copy-start | bytes 196612
  96.6 2.2 %copy-start.5 = (f32[3,40,128]{2,1,0:T(8,128)S(1)}, f32[3,40,128]{2,1,0:T(8,128)}, u32[]{:S(2)}) copy-start(f32[3,40,128]{2,1,0:T(8,128)} %get-tuple-element.17) | copy-start | bytes 184324
  98.1 1.3 %copy-start.1 = (f32[32,1,8,128]{3,2,1,0:T(8,128)S(1)}, f32[32,1,8,128]{3,2,1,0:T(8,128)}, u32[]{:S(2)}) copy-start(f32[32,1,8,128]{3,2,1,0:T(8,128)} %get-tuple-element.14) | copy-start | bytes 393220
  99.5 1.0 copy-start.7
  100.5 0.8 copy-start.6

commit v3 on v2

--- a/solution.py
+++ b/solution.py
@@ -58,10 +58,14 @@
     ga_r,
     x_s,
     x_r,
+    xf_s,
+    xf_r,
     gb_s,
     gb_r,
     w_s,
     w_r,
+    wf_s,
+    wf_r,
     ch_s,
     ch_r,
     mh_s,
@@ -78,6 +82,9 @@
     CO = 128 // D
     RB = tf.shape[1]
     n = 32 // D
+    chip = d // 2
+    core = lax.rem(d, 2)
+    sibling = 2 * chip + 1 - core
     up = lax.rem(z + 1, Z)
     down = lax.rem(z + Z - 1, Z)
     after = lax.rem(d + 1, D)
@@ -104,8 +111,8 @@
 
     local = [
         pltpu.make_async_copy(gt_ref, ggl.at[:, 1], loc.at[0]),
-        pltpu.make_async_copy(xc_ref, xg.at[d], loc.at[1]),
-        pltpu.make_async_copy(ws_ref, wg.at[d], loc.at[2]),
+        pltpu.make_async_copy(xc_ref, xg.at[chip, core], loc.at[1]),
+        pltpu.make_async_copy(ws_ref, wg.at[chip, core], loc.at[2]),
         pltpu.make_async_copy(m_ref, me.at[1:3, 1:5], loc.at[3]),
     ]
     for c in local:
@@ -149,7 +156,19 @@
         c.wait_recv()
         c.wait_send()
 
-    to_plane(lambda e: xc_ref, xg.at[d], x_s, x_r)
+    def to_chips(src, dst, s, r):
+        def one(k, carry):
+            e = lax.rem(chip + k, D // 2)
+            remote(src, dst, s, r, (2 * e + core, z)).start()
+            return carry
+
+        lax.fori_loop(1, D // 2, one, 0)
+
+    def from_chips(whole, s, r):
+        rest = whole.at[pl.ds(0, D // 2 - 1), 0]
+        remote(rest, rest, s, r, (sibling, z)).wait()
+
+    to_chips(xc_ref, xg.at[chip, core], x_s, x_r)
 
     ch = []
     for ai, to_d in ((0, after), (1, d), (2, before)):
@@ -176,7 +195,6 @@
     keep = pltpu.make_async_copy(ggl.at[d], gg.at[d], loc.at[4])
     keep.start()
     to_plane(lambda e: ggl.at[e], gg.at[d], gb_s, gb_r)
-    to_plane(lambda e: ws_ref, wg.at[d], w_s, w_r)
 
     local[3].wait()
     for c in mh:
@@ -234,6 +252,11 @@
     for at in range(2):
         for h in range(4):
             mo_ref[at, h] = outs[at][:, 128 * h : 128 * h + 128].astype(BF16)
+    local[1].wait()
+    from_chips(xg, x_s, x_r)
+    x_on = remote(xg.at[:, core], xg.at[:, core], xf_s, xf_r, (sibling, z))
+    x_on.start()
+    to_chips(ws_ref, wg.at[chip, core], w_s, w_r)
     outs = [None] * 2
     for dd in range(4):
         part = dot(wb_ref[...], columns(dd, 1), NN)
@@ -251,9 +274,9 @@
     from_plane(gg, gb_s, gb_r)
     lanes = lax.broadcasted_iota(jnp.int32, (D, CO, 128), 2)
     first = lanes < 64
-    below = jnp.where(z > 0, gg[:, 0], 0.0)
-    here = gg[:, 1]
-    above = jnp.where(z < Z - 1, gg[:, 2], 0.0)
+    below = jnp.where(z > 0, gg[:, 0].astype(F32), 0.0)
+    here = gg[:, 1].astype(F32)
+    above = jnp.where(z < Z - 1, gg[:, 2].astype(F32), 0.0)
 
     def turned(v, amount):
         return pltpu.roll(v.reshape(D * CO, 128), amount, 1).reshape(D, CO, 128)
@@ -275,8 +298,7 @@
         for c in range(3):
             at = (b * 3 + c) * CO
             tf[1 : D + 1, at : at + CO, :] = shifted[c]
-    local[1].wait()
-    from_plane(xg, x_s, x_r)
+    x_on.wait()
 
     def plane_pair(k, acc):
         s = 2 * k
@@ -287,7 +309,7 @@
             ],
             axis=1,
         )
-        return acc + dot(taps, xg[pl.ds(s, 2)].reshape(256, 128), NN)
+        return acc + dot(taps, xg[k].reshape(256, 128), NN)
 
     acc = lax.fori_loop(0, D // 2, plane_pair, jnp.zeros((3 * RB, 128), F32))
     for a in range(3):
@@ -301,24 +323,29 @@
 
     far = Z // 2
 
-    def hop(way, step):
+    part = zl.shape[1] // 4
+
+    def hop(way, step, q):
         if way == 0:
-            slot = zl.at[lax.rem(z + Z - step, Z)]
+            slot = lax.rem(z + Z - step, Z)
             to = up
         else:
-            slot = zl.at[lax.rem(z + step, Z)]
+            slot = lax.rem(z + step, Z)
             to = down
-        return remote(slot, slot, ring_s.at[way, step], ring_r.at[way, step], (d, to))
+        rows = zl.at[slot, pl.ds(part * q, part)]
+        return remote(
+            rows, rows, ring_s.at[way, q, step], ring_r.at[way, q, step], (d, to)
+        )
+
+    last = (far, far - 1)
 
     def serve(step):
-        if step > 0:
-            hop(0, step - 1).wait()
-            if step - 1 < far - 1:
-                hop(1, step - 1).wait()
-        if step < far:
-            hop(0, step).start()
-        if step < far - 1:
-            hop(1, step).start()
+        for q in range(4):
+            for way in range(2):
+                if 0 < step <= last[way]:
+                    hop(way, step - 1, q).wait_recv()
+                if step < last[way]:
+                    hop(way, step, q).start()
 
     serve(0)
 
@@ -330,7 +357,7 @@
         near = jnp.clip(d + a - 1, 0, D - 1)
         for k, col in ((0, xcol), (1, gcol)):
             if k == 0:
-                centre = xg[near]
+                centre = xg[near // 2, lax.rem(near, 2)]
             else:
                 centre = gc_ref[...] if a == 1 else gd[a // 2]
             low = jnp.where(z > 0, hr[a, 0, k].astype(F32), 0.0)
@@ -346,18 +373,30 @@
                 col[a, :, 128 * c : 128 * c + 128] = v.astype(BF16)
     serve(1)
     local[2].wait()
-    from_plane(wg, w_s, w_r)
+    from_chips(wg, w_s, w_r)
+    w_on = remote(wg.at[:, core], wg.at[:, core], wf_s, wf_r, (sibling, z))
+    w_on.start()
+    for step in range(2, far + 1):
+        serve(step)
+
+    total = zl[0]
+    for s in range(1, Z):
+        total = total + zl[s]
+    cw_ref[...] = (total[: 3 * RB] * coarse_scale).reshape(3, RB, 128)
+    own[...] = (total[3 * RB : 3 * RB + 8 * n] * middle_scale).reshape(n, 8, 128)
+    keep_mg = pltpu.make_async_copy(own, mg.at[d], loc.at[6])
+    keep_mg.start()
+    to_plane(lambda e: own, mg.at[d], mg_s, mg_r)
+    w_on.wait()
 
     def tap(t):
-        w = wg[:, t].astype(F32)
+        w = wg[:, :, t].astype(F32)
         if CO % 8:
-            w = w.reshape(D // 2, 2, CO, 128)
             w = jnp.concatenate([w[:, 0], w[:, 1]], axis=1)
         return w.reshape(128, 128).astype(BF16)
 
     out = jnp.zeros((128, 128), F32)
     dx = jnp.zeros((128, 128), F32)
-    step = 2
     for a in range(3):
         for b in range(3):
             w = [tap((a * 3 + b) * 3 + c) for c in range(3)]
@@ -367,23 +406,13 @@
                 jnp.concatenate(w[::-1], axis=0),
                 NN,
             )
-            if step <= far:
-                serve(step)
-                step += 1
     co_ref[...] = out.astype(BF16)
     cdx_ref[...] = dx.astype(BF16)
-    while step <= far:
-        serve(step)
-        step += 1
-
-    total = zl[0]
-    for s in range(1, Z):
-        total = total + zl[s]
-    cw_ref[...] = (total[: 3 * RB] * coarse_scale).reshape(3, RB, 128)
-    own[...] = (total[3 * RB : 3 * RB + 8 * n] * middle_scale).reshape(n, 8, 128)
-    keep_mg = pltpu.make_async_copy(own, mg.at[d], loc.at[6])
-    keep_mg.start()
-    to_plane(lambda e: own, mg.at[d], mg_s, mg_r)
+    for step in range(far):
+        for q in range(4):
+            for way in range(2):
+                if step < last[way]:
+                    hop(way, step, q).wait_send()
     keep_mg.wait()
     from_plane(mg, mg_s, mg_r)
     mw_ref[...] = mg[...]
@@ -404,7 +433,7 @@
     wb = jnp.transpose(middle_weight[::-1, ::-1, ::-1], (0, 3, 1, 2, 4)).reshape(96, 288)
     xc = coarse_input.reshape(128, 128)
     gc = coarse_cotangent.reshape(128, 128)
-    gt = gc.T.astype(F32).reshape(D, CO, 128)
+    gt = gc.T.reshape(D, CO, 128)
     ws = jnp.swapaxes(coarse_weight, 3, 4).reshape(27, CO, 128)
     dma = pltpu.SemaphoreType.DMA
     vmem = pl.BlockSpec(memory_space=pltpu.VMEM)
@@ -428,10 +457,10 @@
             pltpu.VMEM((32, 8, 128), F32),
             pltpu.VMEM((D, n, 8, 128), F32),
             pltpu.VMEM((n, 8, 128), F32),
-            pltpu.VMEM((D, 128, 128), BF16),
-            pltpu.VMEM((D, 27, CO, 128), BF16),
-            pltpu.VMEM((D, 3, CO, 128), F32),
-            pltpu.VMEM((D, 3, CO, 128), F32),
+            pltpu.VMEM((D // 2, 2, 128, 128), BF16),
+            pltpu.VMEM((D // 2, 2, 27, CO, 128), BF16),
+            pltpu.VMEM((D, 3, CO, 128), BF16),
+            pltpu.VMEM((D, 3, CO, 128), BF16),
             pltpu.VMEM((D + 2, RB, 128), F32),
             pltpu.VMEM((3, 2, 2, 64, 128), BF16),
             pltpu.VMEM((2, 128, 128), BF16),
@@ -448,6 +477,10 @@
             dma,
             dma,
             dma,
+            dma,
+            dma,
+            dma,
+            dma,
             dma((14,)),
             dma((14,)),
             dma((8,)),
@@ -456,8 +489,8 @@
             dma,
             dma,
             dma,
-            dma((2, far)),
-            dma((2, far)),
+            dma((2, 4, far)),
+            dma((2, 4, far)),
         ],
         compiler_params=pltpu.CompilerParams(collective_id=0, has_side_effects=True),
     )(m, wf, wb, xc, gc, gt, ws)

time: 102 us -> 79.6 us (0.78)
  Pallas kernels: 91.3 us -> 68.3 us
  local copies, waits for them, and re-layouts: 8.38 us -> 9.65 us
    pallas_call x1, Pallas kernels: 91.3 us -> 68.3 us  [per_device(): pl.pallas_call(functools.partial(kernel, D, Z, 1.0 / math.sqrt(middle_cel...]
    transpose x0 -> x1, local copies, waits for them, and re-layouts: none -> 1.51 us  [per_device(): gt = gc.T.reshape(D, CO, 128)]
    unnamed x21 -> x19, local copies, waits for them, and re-layouts: 4.98 us -> 4.57 us
where the time goes in v3:
time: 79.6 us; the launch traced here: 79.3 us
  Pallas kernels  68.3 us (86%)
  local copies, waits for them, and re-layouts  9.65 us (12%)
    pallas_call x1, Pallas kernels, per_device(): pl.pallas_call(functools.partial(kernel, D, Z, 1.0 / math.sqrt(middle_cel...  68.3 us
    unnamed x19, local copies, waits for them, and re-layouts  4.57 us

profile of v3, /device:TPU:1, one launch (start us, length us, event | category | flops | bytes accessed | tf_op | source)
XLA Modules:
  0.0 79.3 jit_solution(6599189918492530967)
XLA Ops:
  0.6 0.0 copy-start.3
  0.6 1.5 %copy.31 = bf16[128,128]{1,0:T(8,128)(2,1)} copy(bf16[128,128]{0,1:T(8,128)(2,1)} %bitcast.32) | data formatting | bytes 65536 | tf_op jit(solution)/shard_map/transpose | solution.py:436
  2.1 0.0 copy-done.3
  2.2 0.0 copy-start
  2.2 0.9 %copy_bitcast_fusion = (bf16[2,4,32,128]{3,2,1,0:T(8,128)(2,1)S(1)}, bf16[2,4,32,128]{3,2,1,0:T(8,128)(2,1)S(1)}) fusion(bf16[2,32,4,128]{3,2,1,0:T(4,128)(2,1)S(1)} %copy-done.3, bf16[2,32,4,128]{3,2,1,0:T(4,128)(2,1)} %param.6), kind=kLoop, calls=%fused_computation.3 | loop fusion | bytes 262144 | tf_op jit(solution)/shard_map/transpose | solution.py:430
  3.1 0.7 pad_maximum_fusion.m_ref
  3.7 0.0 copy-done
  3.7 0.2 copy.30
  3.9 0.8 %reshape.52.wb_ref = bf16[96,288]{1,0:T(8,128)(2,1)} reshape(bf16[3,32,3,3,32]{4,3,2,1,0:T(4,128)(2,1)S(1)} %copy.30) | data formatting | bytes 110592 | tf_op jit(solution)/shard_map/reshape | solution.py:433
  4.7 0.2 copy.29
  4.9 0.8 %reshape.51.wf_ref = bf16[96,288]{1,0:T(8,128)(2,1)} reshape(bf16[3,32,3,3,32]{4,3,2,1,0:T(4,128)(2,1)S(1)} %copy.29) | data formatting | bytes 110592 | tf_op jit(solution)/shard_map/reshape | solution.py:432
  5.8 68.3 %shard_map.109 = (bf16[2,4,32,128]{3,2,1,0:T(8,128)(2,1)}, bf16[2,4,32,128]{3,2,1,0:T(8,128)(2,1)}, f32[32,1,8,128]{3,2,1,0:T(8,128)}, bf16[128,128]{1,0:T(8,128...) custom-call(bf16[2,4,64,128]{3,2,1,0:T(8,128)(2,1)} %pad_maximum_fusion.m_ref, bf16[96,288]{1,0:T(8,128)(2,1)} %reshape.51.wf_ref, ...), custom_call_target="tpu_custom_call" | custom-call | tf_op jit(solution)/shard_map/pallas_call | solution.py:440
  74.0 0.0 copy-start.2
  74.0 0.0 copy-start.4
  74.1 1.5 %copy.32 = bf16[2,32,4,128]{3,2,1,0:T(4,128)(2,1)} copy(bf16[2,32,4,128]{3,1,2,0:T(8,128)(2,1)} %bitcast.36) | data formatting | bytes 131072
  75.6 0.0 copy-start.1
  75.6 0.0 copy-done.2
  75.6 0.7 copy.33
  76.3 0.0 copy-done.4
  76.3 0.6 reshape.62
  76.9 0.0 copy-done.1
  76.9 0.0 copy-start.6
  76.9 1.0 %copy.35 = f32[864,32]{1,0:T(8,128)} copy(f32[864,32]{0,1:T(8,128)S(1)} %slice_bitcast_fusion) | data formatting | bytes 221184
  77.9 0.0 copy-done.6
  77.9 0.0 copy-start.5
  77.9 0.6 copy.40
  78.5 0.2 copy-done.5
  78.7 0.6 copy.41
  (3 shorter events, 0.0 us)
Async XLA Ops:
  0.6 1.5 %copy-start.3 = (bf16[2,32,4,128]{3,2,1,0:T(4,128)(2,1)S(1)}, bf16[2,32,4,128]{3,2,1,0:T(4,128)(2,1)}, u32[]{:S(2)}) copy-start(bf16[2,32,4,128]{3,2,1,0:T(4,128)(2,1)} %param.7) | copy-start | bytes 196612
  2.2 1.6 %copy-start = (bf16[3,3,3,32,32]{4,3,2,1,0:T(8,128)(2,1)S(1)}, bf16[3,3,3,32,32]{4,3,2,1,0:T(8,128)(2,1)}, u32[]{:S(2)}) copy-start(bf16[3,3,3,32,32]{4,3,2,1,0:T(8,128)(2,1)} %param.8) | copy-start | bytes 165892
  74.0 1.6 %copy-start.2 = (bf16[2,4,32,128]{3,2,1,0:T(8,128)(2,1)S(1)}, bf16[2,4,32,128]{3,2,1,0:T(8,128)(2,1)}, u32[]{:S(2)}) copy-start(bf16[2,4,32,128]{3,2,1,0:T(8,128)(2,1)} %get-tuple-element.13) | copy-start | bytes 196612
  74.0 2.2 %copy-start.4 = (f32[3,40,128]{2,1,0:T(8,128)S(1)}, f32[3,40,128]{2,1,0:T(8,128)}, u32[]{:S(2)}) copy-start(f32[3,40,128]{2,1,0:T(8,128)} %get-tuple-element.17) | copy-start | bytes 184324
  75.6 1.3 %copy-start.1 = (f32[32,1,8,128]{3,2,1,0:T(8,128)S(1)}, f32[32,1,8,128]{3,2,1,0:T(8,128)}, u32[]{:S(2)}) copy-start(f32[32,1,8,128]{3,2,1,0:T(8,128)} %get-tuple-element.14) | copy-start | bytes 393220
  76.9 1.0 %copy-start.6 = (bf16[128,128]{1,0:T(8,128)(2,1)S(1)}, bf16[128,128]{1,0:T(8,128)(2,1)}, u32[]{:S(2)}) copy-start(bf16[128,128]{1,0:T(8,128)(2,1)} %get-tuple-element.15) | copy-start | bytes 98308
  77.9 0.8 copy-start.5

commit v4 on v3

--- a/solution.py
+++ b/solution.py
@@ -24,9 +24,9 @@
     Z,
     middle_scale,
     coarse_scale,
-    m_ref,
-    wf_ref,
-    wb_ref,
+    mi_ref,
+    mc_ref,
+    mk_ref,
     xc_ref,
     gc_ref,
     gt_ref,
@@ -52,6 +52,7 @@
     xcol,
     gcol,
     zl,
+    zm,
     mg,
     loc,
     ga_s,
@@ -76,6 +77,8 @@
     mg_r,
     ring_s,
     ring_r,
+    turn_s,
+    turn_r,
 ):
     d = lax.axis_index("depth")
     z = lax.axis_index("height")
@@ -102,6 +105,22 @@
         for dd in (before, d, after):
             pl.semaphore_signal(barrier, inc=1, device_id=(dd, zz), device_id_type=MESH)
     lax.fori_loop(1, D, greet, 0)
+
+    taps = [mk_ref[t].astype(F32) for t in range(27)]
+    forward = jnp.concatenate(
+        [
+            jnp.concatenate([taps[9 * a + t].T for t in range(9)], axis=1)
+            for a in range(3)
+        ],
+        axis=0,
+    ).astype(BF16)
+    backward = jnp.concatenate(
+        [
+            jnp.concatenate([taps[26 - 9 * a - t] for t in range(9)], axis=1)
+            for a in range(3)
+        ],
+        axis=0,
+    ).astype(BF16)
     pl.semaphore_wait(barrier, D - 1 + 6)
 
     def remote(src, dst, s, r, to):
@@ -113,7 +132,8 @@
         pltpu.make_async_copy(gt_ref, ggl.at[:, 1], loc.at[0]),
         pltpu.make_async_copy(xc_ref, xg.at[chip, core], loc.at[1]),
         pltpu.make_async_copy(ws_ref, wg.at[chip, core], loc.at[2]),
-        pltpu.make_async_copy(m_ref, me.at[1:3, 1:5], loc.at[3]),
+        pltpu.make_async_copy(mi_ref, me.at[1:3, 1:5, 0:32], loc.at[3]),
+        pltpu.make_async_copy(mc_ref, me.at[1:3, 1:5, 32:64], loc.at[7]),
     ]
     for c in local:
         c.start()
@@ -126,19 +146,21 @@
         c.start()
 
     mh = []
-    for i, (dst, src, to) in enumerate(
-        (
-            (me.at[0, 1:5], m_ref.at[1], (after, z)),
-            (me.at[3, 1:5], m_ref.at[0], (before, z)),
-            (me.at[1:3, 0], m_ref.at[:, 3], (d, up)),
-            (me.at[1:3, 5], m_ref.at[:, 0], (d, down)),
-            (me.at[0, 0], m_ref.at[1, 3], (after, up)),
-            (me.at[0, 5], m_ref.at[1, 0], (after, down)),
-            (me.at[3, 0], m_ref.at[0, 3], (before, up)),
-            (me.at[3, 5], m_ref.at[0, 0], (before, down)),
-        )
-    ):
-        mh.append(remote(src, dst, mh_s.at[i], mh_r.at[i], to))
+    for k, ref in ((0, mi_ref), (1, mc_ref)):
+        part = slice(32 * k, 32 * k + 32)
+        for i, (dst, src, to) in enumerate(
+            (
+                (me.at[0, 1:5, part], ref.at[1], (after, z)),
+                (me.at[3, 1:5, part], ref.at[0], (before, z)),
+                (me.at[1:3, 0, part], ref.at[:, 3], (d, up)),
+                (me.at[1:3, 5, part], ref.at[:, 0], (d, down)),
+                (me.at[0, 0, part], ref.at[1, 3], (after, up)),
+                (me.at[0, 5, part], ref.at[1, 0], (after, down)),
+                (me.at[3, 0, part], ref.at[0, 3], (before, up)),
+                (me.at[3, 5, part], ref.at[0, 0], (before, down)),
+            )
+        ):
+            mh.append(remote(src, dst, mh_s.at[k, i], mh_r.at[k, i], to))
     for c in mh:
         c.start()
 
@@ -197,6 +219,7 @@
     to_plane(lambda e: ggl.at[e], gg.at[d], gb_s, gb_r)
 
     local[3].wait()
+    local[4].wait()
     for c in mh:
         c.wait()
     depth_ok = (d > 0, None, None, d < D - 1)
@@ -232,7 +255,7 @@
     outs = [None] * 2
     for dd in range(4):
         cols = columns(dd, 0)
-        part = dot(wf_ref[...], cols, NN)
+        part = dot(forward, cols, NN)
         for a in range(3):
             at = dd - a
             if 0 <= at < 2:
@@ -257,9 +280,72 @@
     x_on = remote(xg.at[:, core], xg.at[:, core], xf_s, xf_r, (sibling, z))
     x_on.start()
     to_chips(ws_ref, wg.at[chip, core], w_s, w_r)
+    far = Z // 2
+
+    third = zl.shape[1] // 3
+
+    def hop(way, step, q):
+        if way == 0:
+            slot = lax.rem(z + Z - step, Z)
+            to = up
+        else:
+            slot = lax.rem(z + step, Z)
+            to = down
+        rows = zl.at[slot, pl.ds(third * q, third)]
+        return remote(
+            rows, rows, ring_s.at[way, q, step], ring_r.at[way, q, step], (d, to)
+        )
+
+    last = (far, far - 1)
+
+    def serve(step):
+        for q in range(3):
+            for way in range(2):
+                if 0 < step <= last[way]:
+                    hop(way, step - 1, q).wait_recv()
+                if step < last[way]:
+                    hop(way, step, q).start()
+
+    def turn(way, step):
+        slot = lax.rem(z + Z - step, Z) if way == 0 else lax.rem(z + step, Z)
+        rows = zm.at[slot]
+        to = down if way else up
+        return remote(rows, rows, turn_s.at[way, step], turn_r.at[way, step], (d, to))
+
+    def serve_middle(step):
+        for way in range(2):
+            if 0 < step <= last[way]:
+                turn(way, step - 1).wait_recv()
+            if step < last[way]:
+                turn(way, step).start()
+
+    keep_mr.wait()
+    from_plane(mrl, mr_s, mr_r)
+    total = mrl[0]
+    for e in range(1, D):
+        total = total + mrl[e]
+    zm[z] = total.reshape(8 * n, 128)
+    served = []
+    last_gather = pltpu.make_async_copy(own, mg.at[d], loc.at[6])
+
+    def advance():
+        step = len(served)
+        if step > far:
+            return
+        served.append(step)
+        serve_middle(step)
+        if step == far:
+            whole = zm[0]
+            for s in range(1, Z):
+                whole = whole + zm[s]
+            own[...] = (whole * middle_scale).reshape(n, 8, 128)
+            last_gather.start()
+            to_plane(lambda e: own, mg.at[d], mg_s, mg_r)
+
+    advance()
     outs = [None] * 2
     for dd in range(4):
-        part = dot(wb_ref[...], columns(dd, 1), NN)
+        part = dot(backward, columns(dd, 1), NN)
         for a in range(3):
             at = dd - a
             if 0 <= at < 2:
@@ -268,6 +354,8 @@
     for at in range(2):
         for h in range(4):
             mdx_ref[at, h] = outs[at][:, 128 * h : 128 * h + 128].astype(BF16)
+
+    advance()
 
     tf[...] = jnp.zeros(tf.shape, F32)
     keep.wait()
@@ -298,6 +386,7 @@
         for c in range(3):
             at = (b * 3 + c) * CO
             tf[1 : D + 1, at : at + CO, :] = shifted[c]
+    advance()
     x_on.wait()
 
     def plane_pair(k, acc):
@@ -314,40 +403,9 @@
     acc = lax.fori_loop(0, D // 2, plane_pair, jnp.zeros((3 * RB, 128), F32))
     for a in range(3):
         zl[z, a * RB : (a + 1) * RB, :] = acc[(2 - a) * RB : (3 - a) * RB]
-    keep_mr.wait()
-    from_plane(mrl, mr_s, mr_r)
-    total = mrl[0]
-    for e in range(1, D):
-        total = total + mrl[e]
-    zl[z, 3 * RB : 3 * RB + 8 * n, :] = total.reshape(8 * n, 128)
-
-    far = Z // 2
-
-    part = zl.shape[1] // 4
-
-    def hop(way, step, q):
-        if way == 0:
-            slot = lax.rem(z + Z - step, Z)
-            to = up
-        else:
-            slot = lax.rem(z + step, Z)
-            to = down
-        rows = zl.at[slot, pl.ds(part * q, part)]
-        return remote(
-            rows, rows, ring_s.at[way, q, step], ring_r.at[way, q, step], (d, to)
-        )
-
-    last = (far, far - 1)
-
-    def serve(step):
-        for q in range(4):
-            for way in range(2):
-                if 0 < step <= last[way]:
-                    hop(way, step - 1, q).wait_recv()
-                if step < last[way]:
-                    hop(way, step, q).start()
 
     serve(0)
+    advance()
 
     for c in ch:
         c.wait()
@@ -372,21 +430,19 @@
             for c, v in enumerate((prev, rows, nxt)):
                 col[a, :, 128 * c : 128 * c + 128] = v.astype(BF16)
     serve(1)
+    advance()
     local[2].wait()
     from_chips(wg, w_s, w_r)
     w_on = remote(wg.at[:, core], wg.at[:, core], wf_s, wf_r, (sibling, z))
     w_on.start()
     for step in range(2, far + 1):
         serve(step)
+        advance()
 
     total = zl[0]
     for s in range(1, Z):
         total = total + zl[s]
-    cw_ref[...] = (total[: 3 * RB] * coarse_scale).reshape(3, RB, 128)
-    own[...] = (total[3 * RB : 3 * RB + 8 * n] * middle_scale).reshape(n, 8, 128)
-    keep_mg = pltpu.make_async_copy(own, mg.at[d], loc.at[6])
-    keep_mg.start()
-    to_plane(lambda e: own, mg.at[d], mg_s, mg_r)
+    cw_ref[...] = (total * coarse_scale).reshape(3, RB, 128)
     w_on.wait()
 
     def tap(t):
@@ -409,11 +465,15 @@
     co_ref[...] = out.astype(BF16)
     cdx_ref[...] = dx.astype(BF16)
     for step in range(far):
-        for q in range(4):
+        for q in range(3):
             for way in range(2):
                 if step < last[way]:
                     hop(way, step, q).wait_send()
-    keep_mg.wait()
+    for step in range(far):
+        for way in range(2):
+            if step < last[way]:
+                turn(way, step).wait_send()
+    last_gather.wait()
     from_plane(mg, mg_s, mg_r)
     mw_ref[...] = mg[...]
 
@@ -422,15 +482,13 @@
     CO = 128 // D
     RB = -(-9 * CO // 8) * 8
     n = 32 // D
-    R = 3 * RB + 8 * n
+    R = 3 * RB
     far = Z // 2
     middle_cells = middle_input.shape[0] * D * middle_input.shape[2] * Z * middle_input.shape[3]
     coarse_cells = coarse_input.shape[0] * D * coarse_input.shape[1] * Z * coarse_input.shape[2]
-    m = jnp.concatenate(
-        [jnp.swapaxes(middle_input, 1, 2), jnp.swapaxes(middle_cotangent, 1, 2)], axis=2
-    )
-    wf = jnp.transpose(middle_weight, (0, 4, 1, 2, 3)).reshape(96, 288)
-    wb = jnp.transpose(middle_weight[::-1, ::-1, ::-1], (0, 3, 1, 2, 4)).reshape(96, 288)
+    mi = jnp.swapaxes(middle_input, 1, 2)
+    mc = jnp.swapaxes(middle_cotangent, 1, 2)
+    mk = middle_weight.reshape(27, 32, 32)
     xc = coarse_input.reshape(128, 128)
     gc = coarse_cotangent.reshape(128, 128)
     gt = gc.T.reshape(D, CO, 128)
@@ -467,8 +525,9 @@
             pltpu.VMEM((3, 256, 384), BF16),
             pltpu.VMEM((3, 256, 384), BF16),
             pltpu.VMEM((Z, R, 128), F32),
+            pltpu.VMEM((Z, 8 * n, 128), F32),
             pltpu.VMEM((D, n, 8, 128), F32),
-            dma((7,)),
+            dma((8,)),
             dma((2,)),
             dma((2,)),
             dma,
@@ -483,17 +542,19 @@
             dma,
             dma((14,)),
             dma((14,)),
-            dma((8,)),
-            dma((8,)),
-            dma,
-            dma,
-            dma,
-            dma,
-            dma((2, 4, far)),
-            dma((2, 4, far)),
+            dma((2, 8)),
+            dma((2, 8)),
+            dma,
+            dma,
+            dma,
+            dma,
+            dma((2, 3, far)),
+            dma((2, 3, far)),
+            dma((2, far)),
+            dma((2, far)),
         ],
         compiler_params=pltpu.CompilerParams(collective_id=0, has_side_effects=True),
-    )(m, wf, wb, xc, gc, gt, ws)
+    )(mi, mc, mk, xc, gc, gt, ws)
     middle_out = jnp.swapaxes(mo, 1, 2)
     middle_dx = jnp.swapaxes(mdx, 1, 2)
     tiles = mw.reshape(32, 8, 128)[:28].reshape(4, 7, 8, 128)

time: 79.6 us -> 78 us (0.980)
  the two profiles are of different devices: /device:TPU:1 before, /device:TPU:8 now
where the time goes in v4:
time: 78 us; the launch traced here: 77.6 us
  Pallas kernels  68.7 us (88%)
  local copies, waits for them, and re-layouts  8.24 us (11%)
    pallas_call x1, Pallas kernels, per_device(): pl.pallas_call(functools.partial(kernel, D, Z, 1.0 / math.sqrt(middle_cel...  68.7 us
    unnamed x17, local copies, waits for them, and re-layouts  4.56 us

profile of v4, /device:TPU:8, one launch (start us, length us, event | category | flops | bytes accessed | tf_op | source)
XLA Modules:
  0.0 77.6 jit_solution(9742142785812933191)
XLA Ops:
  0.6 0.0 copy-start.2
  0.6 1.5 %copy.25 = bf16[128,128]{1,0:T(8,128)(2,1)} copy(bf16[128,128]{0,1:T(8,128)(2,1)} %bitcast.30) | data formatting | bytes 65536 | tf_op jit(solution)/shard_map/transpose | solution.py:494
  2.1 0.0 copy-done.2
  2.2 1.5 %copy_bitcast_fusion = (bf16[2,4,32,128]{3,2,1,0:T(8,128)(2,1)}, bf16[2,4,32,128]{3,2,1,0:T(8,128)(2,1)}) fusion(bf16[2,32,4,128]{3,2,1,0:T(4,128)(2,1)S(1)} %copy-done.2, bf16[2,32,4,128]{3,2,1,0:T(4,128)(2,1)} %param.6), kind=kLoop, calls=%fused_computation.1 | loop fusion | bytes 262144 | tf_op jit(solution)/shard_map/transpose | solution.py:490
  3.7 68.7 %shard_map.109 = (bf16[2,4,32,128]{3,2,1,0:T(8,128)(2,1)}, bf16[2,4,32,128]{3,2,1,0:T(8,128)(2,1)}, f32[32,1,8,128]{3,2,1,0:T(8,128)}, bf16[128,128]{1,0:T(8,128...) custom-call(bf16[2,4,32,128]{3,2,1,0:T(8,128)(2,1)} %get-tuple-element.37.mi_ref, ...), custom_call_target="tpu_custom_call" | custom-call | tf_op jit(solution)/shard_map/pallas_call | solution.py:498
  72.4 0.0 copy-start.1
  72.4 0.0 copy-start.3
  72.4 1.5 %copy.26 = bf16[2,32,4,128]{3,2,1,0:T(4,128)(2,1)} copy(bf16[2,32,4,128]{3,1,2,0:T(8,128)(2,1)} %bitcast.34) | data formatting | bytes 131072
  73.9 0.0 copy-start
  73.9 0.0 copy-done.1
  73.9 0.7 copy.27
  74.6 0.0 copy-done.3
  74.6 0.6 reshape.58
  75.2 0.0 copy-done
  75.3 0.0 copy-start.5
  75.3 1.0 %copy.29 = f32[864,32]{1,0:T(8,128)} copy(f32[864,32]{0,1:T(8,128)S(1)} %slice_bitcast_fusion) | data formatting | bytes 221184
  76.2 0.0 copy-done.5
  76.2 0.0 copy-start.4
  76.2 0.6 copy.34
  76.9 0.2 copy-done.4
  77.0 0.6 copy.35
  (2 shorter events, 0.0 us)
Async XLA Ops:
  0.6 1.5 %copy-start.2 = (bf16[2,32,4,128]{3,2,1,0:T(4,128)(2,1)S(1)}, bf16[2,32,4,128]{3,2,1,0:T(4,128)(2,1)}, u32[]{:S(2)}) copy-start(bf16[2,32,4,128]{3,2,1,0:T(4,128)(2,1)} %param.7) | copy-start | bytes 196612
  72.4 1.6 %copy-start.1 = (bf16[2,4,32,128]{3,2,1,0:T(8,128)(2,1)S(1)}, bf16[2,4,32,128]{3,2,1,0:T(8,128)(2,1)}, u32[]{:S(2)}) copy-start(bf16[2,4,32,128]{3,2,1,0:T(8,128)(2,1)} %get-tuple-element.13) | copy-start | bytes 196612
  72.4 2.2 %copy-start.3 = (f32[3,40,128]{2,1,0:T(8,128)S(1)}, f32[3,40,128]{2,1,0:T(8,128)}, u32[]{:S(2)}) copy-start(f32[3,40,128]{2,1,0:T(8,128)} %get-tuple-element.17) | copy-start | bytes 184324
  73.9 1.3 %copy-start = (f32[32,1,8,128]{3,2,1,0:T(8,128)S(1)}, f32[32,1,8,128]{3,2,1,0:T(8,128)}, u32[]{:S(2)}) copy-start(f32[32,1,8,128]{3,2,1,0:T(8,128)} %get-tuple-element.14) | copy-start | bytes 393220
  75.3 1.0 %copy-start.5 = (bf16[128,128]{1,0:T(8,128)(2,1)S(1)}, bf16[128,128]{1,0:T(8,128)(2,1)}, u32[]{:S(2)}) copy-start(bf16[128,128]{1,0:T(8,128)(2,1)} %get-tuple-element.15) | copy-start | bytes 98308
  76.2 0.8 copy-start.4

commit v5 on v4

--- a/solution.py
+++ b/solution.py
@@ -51,7 +51,10 @@
     gd,
     xcol,
     gcol,
+    za,
+    zp,
     zl,
+    fin,
     zm,
     mg,
     loc,
@@ -79,6 +82,8 @@
     ring_r,
     turn_s,
     turn_r,
+    pair_s,
+    pair_r,
 ):
     d = lax.axis_index("depth")
     z = lax.axis_index("height")
@@ -92,6 +97,11 @@
     down = lax.rem(z + Z - 1, Z)
     after = lax.rem(d + 1, D)
     before = lax.rem(d + D - 1, D)
+    up_two = lax.rem(z + 2, Z)
+    down_two = lax.rem(z + Z - 2, Z)
+    pair = z // 2
+    side = lax.rem(z, 2)
+    other = z + 1 - 2 * side
 
     barrier = pltpu.get_barrier_semaphore()
 
@@ -104,6 +114,8 @@
     for zz in (up, down):
         for dd in (before, d, after):
             pl.semaphore_signal(barrier, inc=1, device_id=(dd, zz), device_id_type=MESH)
+    for zz in (up_two, down_two):
+        pl.semaphore_signal(barrier, inc=1, device_id=(d, zz), device_id_type=MESH)
     lax.fori_loop(1, D, greet, 0)
 
     taps = [mk_ref[t].astype(F32) for t in range(27)]
@@ -121,7 +133,7 @@
         ],
         axis=0,
     ).astype(BF16)
-    pl.semaphore_wait(barrier, D - 1 + 6)
+    pl.semaphore_wait(barrier, D - 1 + 8)
 
     def remote(src, dst, s, r, to):
         return pltpu.make_async_remote_copy(
@@ -280,44 +292,53 @@
     x_on = remote(xg.at[:, core], xg.at[:, core], xf_s, xf_r, (sibling, z))
     x_on.start()
     to_chips(ws_ref, wg.at[chip, core], w_s, w_r)
-    far = Z // 2
-
-    third = zl.shape[1] // 3
+    far = Z // 4
+    last = (far, far - 1)
+    half = zl.shape[1] // 2
 
     def hop(way, step, q):
-        if way == 0:
-            slot = lax.rem(z + Z - step, Z)
-            to = up
-        else:
-            slot = lax.rem(z + step, Z)
-            to = down
-        rows = zl.at[slot, pl.ds(third * q, third)]
+        slot = lax.rem(pair + (step if way else Z // 2 - step), Z // 2)
+        rows = zl.at[slot, pl.ds(half * q, half)]
+        to = down_two if way else up_two
         return remote(
             rows, rows, ring_s.at[way, q, step], ring_r.at[way, q, step], (d, to)
         )
 
-    last = (far, far - 1)
-
     def serve(step):
-        for q in range(3):
+        for q in range(2):
             for way in range(2):
                 if 0 < step <= last[way]:
                     hop(way, step - 1, q).wait_recv()
                 if step < last[way]:
                     hop(way, step, q).start()
 
-    def turn(way, step):
-        slot = lax.rem(z + Z - step, Z) if way == 0 else lax.rem(z + step, Z)
+    def turn(way, hops, step):
+        slot = lax.rem(z + (2 * step if way else Z - 2 * step), Z)
         rows = zm.at[slot]
-        to = down if way else up
-        return remote(rows, rows, turn_s.at[way, step], turn_r.at[way, step], (d, to))
+        to = ((up, down), (up_two, down_two))[hops - 1][way]
+        return remote(
+            rows, rows, turn_s.at[way, hops - 1, step], turn_r.at[way, hops - 1, step], (d, to)
+        )
+
+    def turns(step):
+        return [
+            (way, hops, step)
+            for way in range(2)
+            for hops in (2, 1)
+            if 0 <= step < far and 2 * step + hops <= Z // 2 - way
+        ]
 
     def serve_middle(step):
-        for way in range(2):
-            if 0 < step <= last[way]:
-                turn(way, step - 1).wait_recv()
-            if step < last[way]:
-                turn(way, step).start()
+        for t in turns(step - 1):
+            if t[1] == 2:
+                turn(*t).wait_recv()
+        for t in turns(step):
+            turn(*t).start()
+        if step == far:
+            for k in range(far):
+                for t in turns(k):
+                    if t[1] == 1:
+                        turn(*t).wait_recv()
 
     keep_mr.wait()
     from_plane(mrl, mr_s, mr_r)
@@ -401,10 +422,13 @@
         return acc + dot(taps, xg[k].reshape(256, 128), NN)
 
     acc = lax.fori_loop(0, D // 2, plane_pair, jnp.zeros((3 * RB, 128), F32))
-    for a in range(3):
-        zl[z, a * RB : (a + 1) * RB, :] = acc[(2 - a) * RB : (3 - a) * RB]
-
-    serve(0)
+    rows = [acc[(2 - a) * RB : (3 - a) * RB] for a in range(3)]
+    spare = 2 * za.shape[1] - 3 * RB
+    if spare:
+        rows.append(jnp.zeros((spare, 128), F32))
+    za[...] = jnp.concatenate(rows, axis=0).reshape(za.shape)
+    share = remote(za.at[1 - side], zp, pair_s.at[0], pair_r.at[0], (d, other))
+    share.start()
     advance()
 
     for c in ch:
@@ -429,20 +453,24 @@
             nxt = jnp.where(place == 63, 0.0, pltpu.roll(rows, 255, 0))
             for c, v in enumerate((prev, rows, nxt)):
                 col[a, :, 128 * c : 128 * c + 128] = v.astype(BF16)
-    serve(1)
+    share.wait()
+    zl[pair] = za[side] + zp[...]
+    serve(0)
     advance()
     local[2].wait()
     from_chips(wg, w_s, w_r)
     w_on = remote(wg.at[:, core], wg.at[:, core], wf_s, wf_r, (sibling, z))
     w_on.start()
-    for step in range(2, far + 1):
+    for step in range(1, far + 1):
         serve(step)
         advance()
 
     total = zl[0]
-    for s in range(1, Z):
+    for s in range(1, Z // 2):
         total = total + zl[s]
-    cw_ref[...] = (total * coarse_scale).reshape(3, RB, 128)
+    fin[side] = total * coarse_scale
+    swap = remote(fin.at[side], fin.at[side], pair_s.at[1], pair_r.at[1], (d, other))
+    swap.start()
     w_on.wait()
 
     def tap(t):
@@ -464,15 +492,15 @@
             )
     co_ref[...] = out.astype(BF16)
     cdx_ref[...] = dx.astype(BF16)
+    swap.wait()
+    cw_ref[...] = fin[...].reshape(2 * fin.shape[1], 128)[: 3 * RB].reshape(3, RB, 128)
     for step in range(far):
-        for q in range(3):
+        for q in range(2):
             for way in range(2):
                 if step < last[way]:
                     hop(way, step, q).wait_send()
-    for step in range(far):
-        for way in range(2):
-            if step < last[way]:
-                turn(way, step).wait_send()
+        for t in turns(step):
+            turn(*t).wait_send()
     last_gather.wait()
     from_plane(mg, mg_s, mg_r)
     mw_ref[...] = mg[...]
@@ -482,8 +510,8 @@
     CO = 128 // D
     RB = -(-9 * CO // 8) * 8
     n = 32 // D
-    R = 3 * RB
-    far = Z // 2
+    H = -(-3 * RB // 16) * 8
+    far = Z // 4
     middle_cells = middle_input.shape[0] * D * middle_input.shape[2] * Z * middle_input.shape[3]
     coarse_cells = coarse_input.shape[0] * D * coarse_input.shape[1] * Z * coarse_input.shape[2]
     mi = jnp.swapaxes(middle_input, 1, 2)
@@ -524,7 +552,10 @@
             pltpu.VMEM((2, 128, 128), BF16),
             pltpu.VMEM((3, 256, 384), BF16),
             pltpu.VMEM((3, 256, 384), BF16),
-            pltpu.VMEM((Z, R, 128), F32),
+            pltpu.VMEM((2, H, 128), F32),
+            pltpu.VMEM((H, 128), F32),
+            pltpu.VMEM((Z // 2, H, 128), F32),
+            pltpu.VMEM((2, H, 128), F32),
             pltpu.VMEM((Z, 8 * n, 128), F32),
             pltpu.VMEM((D, n, 8, 128), F32),
             dma((8,)),
@@ -548,10 +579,12 @@
             dma,
             dma,
             dma,
-            dma((2, 3, far)),
-            dma((2, 3, far)),
-            dma((2, far)),
-            dma((2, far)),
+            dma((2, 2, far)),
+            dma((2, 2, far)),
+            dma((2, 2, far)),
+            dma((2, 2, far)),
+            dma((2,)),
+            dma((2,)),
         ],
         compiler_params=pltpu.CompilerParams(collective_id=0, has_side_effects=True),
     )(mi, mc, mk, xc, gc, gt, ws)

time: 78 us -> 73.5 us (0.942)
  the two profiles are of different devices: /device:TPU:8 before, /device:TPU:4 now
where the time goes in v5:
time: 73.5 us; the launch traced here: 73.1 us
  Pallas kernels  64.2 us (87%)
  local copies, waits for them, and re-layouts  8.24 us (11%)
    pallas_call x1, Pallas kernels, per_device(): pl.pallas_call(functools.partial(kernel, D, Z, 1.0 / math.sqrt(middle_cel...  64.2 us
    unnamed x17, local copies, waits for them, and re-layouts  4.56 us
    transpose x1, local copies, waits for them, and re-layouts, per_device(): mc = jnp.swapaxes(middle_cotangent, 1, 2)  1.51 us
    transpose x1, local copies, waits for them, and re-layouts, per_device(): gt = gc.T.reshape(D, CO, 128)  1.51 us

profile of v5, /device:TPU:4, one launch (start us, length us, event | category | flops | bytes accessed | tf_op | source)
XLA Modules:
  0.0 73.1 jit_solution(6095691788478067798)
XLA Ops:
  0.6 0.0 copy-start.2
  0.6 1.5 %copy.25 = bf16[128,128]{1,0:T(8,128)(2,1)} copy(bf16[128,128]{0,1:T(8,128)(2,1)} %bitcast.30) | data formatting | bytes 65536 | tf_op jit(solution)/shard_map/transpose | solution.py:522
  2.1 0.0 copy-done.2
  2.2 1.5 %copy_bitcast_fusion = (bf16[2,4,32,128]{3,2,1,0:T(8,128)(2,1)}, bf16[2,4,32,128]{3,2,1,0:T(8,128)(2,1)}) fusion(bf16[2,32,4,128]{3,2,1,0:T(4,128)(2,1)S(1)} %copy-done.2, bf16[2,32,4,128]{3,2,1,0:T(4,128)(2,1)} %param.6), kind=kLoop, calls=%fused_computation.1 | loop fusion | bytes 262144 | tf_op jit(solution)/shard_map/transpose | solution.py:518
  3.7 64.2 %shard_map.109 = (bf16[2,4,32,128]{3,2,1,0:T(8,128)(2,1)}, bf16[2,4,32,128]{3,2,1,0:T(8,128)(2,1)}, f32[32,1,8,128]{3,2,1,0:T(8,128)}, bf16[128,128]{1,0:T(8,128...) custom-call(bf16[2,4,32,128]{3,2,1,0:T(8,128)(2,1)} %get-tuple-element.37.mi_ref, ...), custom_call_target="tpu_custom_call" | custom-call | tf_op jit(solution)/shard_map/pallas_call | solution.py:526
  67.9 0.0 copy-start.1
  67.9 0.0 copy-start.3
  67.9 1.5 %copy.26 = bf16[2,32,4,128]{3,2,1,0:T(4,128)(2,1)} copy(bf16[2,32,4,128]{3,1,2,0:T(8,128)(2,1)} %bitcast.34) | data formatting | bytes 131072
  69.4 0.0 copy-start
  69.4 0.0 copy-done.1
  69.4 0.7 copy.27
  70.1 0.0 copy-done.3
  70.1 0.6 reshape.58
  70.7 0.0 copy-done
  70.8 0.0 copy-start.5
  70.8 1.0 %copy.29 = f32[864,32]{1,0:T(8,128)} copy(f32[864,32]{0,1:T(8,128)S(1)} %slice_bitcast_fusion) | data formatting | bytes 221184
  71.7 0.0 copy-done.5
  71.7 0.0 copy-start.4
  71.7 0.6 copy.34
  72.3 0.2 copy-done.4
  72.5 0.6 copy.35
  (2 shorter events, 0.0 us)
Async XLA Ops:
  0.6 1.5 %copy-start.2 = (bf16[2,32,4,128]{3,2,1,0:T(4,128)(2,1)S(1)}, bf16[2,32,4,128]{3,2,1,0:T(4,128)(2,1)}, u32[]{:S(2)}) copy-start(bf16[2,32,4,128]{3,2,1,0:T(4,128)(2,1)} %param.7) | copy-start | bytes 196612
  67.9 1.6 %copy-start.1 = (bf16[2,4,32,128]{3,2,1,0:T(8,128)(2,1)S(1)}, bf16[2,4,32,128]{3,2,1,0:T(8,128)(2,1)}, u32[]{:S(2)}) copy-start(bf16[2,4,32,128]{3,2,1,0:T(8,128)(2,1)} %get-tuple-element.13) | copy-start | bytes 196612
  67.9 2.2 %copy-start.3 = (f32[3,40,128]{2,1,0:T(8,128)S(1)}, f32[3,40,128]{2,1,0:T(8,128)}, u32[]{:S(2)}) copy-start(f32[3,40,128]{2,1,0:T(8,128)} %get-tuple-element.17) | copy-start | bytes 184324
  69.4 1.3 %copy-start = (f32[32,1,8,128]{3,2,1,0:T(8,128)S(1)}, f32[32,1,8,128]{3,2,1,0:T(8,128)}, u32[]{:S(2)}) copy-start(f32[32,1,8,128]{3,2,1,0:T(8,128)} %get-tuple-element.14) | copy-start | bytes 393220
  70.8 1.0 %copy-start.5 = (bf16[128,128]{1,0:T(8,128)(2,1)S(1)}, bf16[128,128]{1,0:T(8,128)(2,1)}, u32[]{:S(2)}) copy-start(bf16[128,128]{1,0:T(8,128)(2,1)} %get-tuple-element.15) | copy-start | bytes 98308
  71.7 0.8 %copy-start.4 = (bf16[128,128]{1,0:T(8,128)(2,1)S(1)}, bf16[128,128]{1,0:T(8,128)(2,1)}, u32[]{:S(2)}) copy-start(bf16[128,128]{1,0:T(8,128)(2,1)} %get-tuple-element.16) | copy-start | bytes 98308

commit v6 on v5

--- a/solution.py
+++ b/solution.py
@@ -32,10 +32,8 @@
     gt_ref,
     ws_ref,
     mo_ref,
-    mdx_ref,
     mw_ref,
     co_ref,
-    cdx_ref,
     cw_ref,
     me,
     mv,
@@ -286,7 +284,7 @@
     to_plane(lambda e: mr.at[pl.ds(e * n, n)], mrl.at[d], mr_s, mr_r)
     for at in range(2):
         for h in range(4):
-            mo_ref[at, h] = outs[at][:, 128 * h : 128 * h + 128].astype(BF16)
+            mo_ref[0, at, h] = outs[at][:, 128 * h : 128 * h + 128].astype(BF16)
     local[1].wait()
     from_chips(xg, x_s, x_r)
     x_on = remote(xg.at[:, core], xg.at[:, core], xf_s, xf_r, (sibling, z))
@@ -374,9 +372,7 @@
                 outs[at] = p if outs[at] is None else outs[at] + p
     for at in range(2):
         for h in range(4):
-            mdx_ref[at, h] = outs[at][:, 128 * h : 128 * h + 128].astype(BF16)
-
-    advance()
+            mo_ref[1, at, h] = outs[at][:, 128 * h : 128 * h + 128].astype(BF16)
 
     tf[...] = jnp.zeros(tf.shape, F32)
     keep.wait()
@@ -407,7 +403,6 @@
         for c in range(3):
             at = (b * 3 + c) * CO
             tf[1 : D + 1, at : at + CO, :] = shifted[c]
-    advance()
     x_on.wait()
 
     def plane_pair(k, acc):
@@ -490,8 +485,8 @@
                 jnp.concatenate(w[::-1], axis=0),
                 NN,
             )
-    co_ref[...] = out.astype(BF16)
-    cdx_ref[...] = dx.astype(BF16)
+    co_ref[0] = out.astype(BF16)
+    co_ref[1] = dx.astype(BF16)
     swap.wait()
     cw_ref[...] = fin[...].reshape(2 * fin.shape[1], 128)[: 3 * RB].reshape(3, RB, 128)
     for step in range(far):
@@ -523,20 +518,18 @@
     ws = jnp.swapaxes(coarse_weight, 3, 4).reshape(27, CO, 128)
     dma = pltpu.SemaphoreType.DMA
     vmem = pl.BlockSpec(memory_space=pltpu.VMEM)
-    mo, mdx, mw, co, cdx, cw = pl.pallas_call(
+    mo, mw, co, cw = pl.pallas_call(
         functools.partial(
             kernel, D, Z, 1.0 / math.sqrt(middle_cells), 1.0 / math.sqrt(coarse_cells)
         ),
         out_shape=(
-            jax.ShapeDtypeStruct((2, 4, 32, 128), BF16),
-            jax.ShapeDtypeStruct((2, 4, 32, 128), BF16),
+            jax.ShapeDtypeStruct((2, 2, 4, 32, 128), BF16),
             jax.ShapeDtypeStruct((D, n, 8, 128), F32),
-            jax.ShapeDtypeStruct((128, 128), BF16),
-            jax.ShapeDtypeStruct((128, 128), BF16),
+            jax.ShapeDtypeStruct((2, 128, 128), BF16),
             jax.ShapeDtypeStruct((3, RB, 128), F32),
         ),
         in_specs=[vmem] * 7,
-        out_specs=(vmem,) * 6,
+        out_specs=(vmem,) * 4,
         scratch_shapes=[
             pltpu.VMEM((4, 6, 64, 128), BF16),
             pltpu.VMEM((4, 6, 2, 96, 128), BF16),
@@ -588,8 +581,8 @@
         ],
         compiler_params=pltpu.CompilerParams(collective_id=0, has_side_effects=True),
     )(mi, mc, mk, xc, gc, gt, ws)
-    middle_out = jnp.swapaxes(mo, 1, 2)
-    middle_dx = jnp.swapaxes(mdx, 1, 2)
+    middle_out = jnp.swapaxes(mo[0], 1, 2)
+    middle_dx = jnp.swapaxes(mo[1], 1, 2)
     tiles = mw.reshape(32, 8, 128)[:28].reshape(4, 7, 8, 128)
     flat = jnp.transpose(tiles, (0, 2, 1, 3)).reshape(32, 896)[:, :864]
     middle_dw = flat.T.reshape(3, 3, 3, 32, 32)
@@ -598,8 +591,8 @@
         middle_out,
         middle_dx,
         middle_dw,
-        co.reshape(coarse_input.shape),
-        cdx.reshape(coarse_input.shape),
+        co[0].reshape(coarse_input.shape),
+        co[1].reshape(coarse_input.shape),
         coarse_dw,
     )
 

time: 73.5 us -> 65.7 us (0.89)
  the two profiles are of different devices: /device:TPU:4 before, /device:TPU:8 now
where the time goes in v6:
time: 65.7 us; the launch traced here: 65.4 us
  Pallas kernels  57 us (87%)
  local copies, waits for them, and re-layouts  7.64 us (12%)
  between operations  0.68 us (1%)
    pallas_call x1, Pallas kernels, per_device(): pl.pallas_call(functools.partial(kernel, D, Z, 1.0 / math.sqrt(middle_cel...  57 us
    unnamed x11, local copies, waits for them, and re-layouts  2.46 us
    transpose x1, local copies, waits for them, and re-layouts, per_device(): mc = jnp.swapaxes(middle_cotangent, 1, 2)  1.51 us
    transpose x1, local copies, waits for them, and re-layouts, per_device(): gt = gc.T.reshape(D, CO, 128)  1.51 us

profile of v6, /device:TPU:8, one launch (start us, length us, event | category | flops | bytes accessed | tf_op | source)
XLA Modules:
  0.0 65.4 jit_solution(4528943634886878881)
XLA Ops:
  0.6 0.0 copy-start.2
  0.6 1.5 %copy.25 = bf16[128,128]{1,0:T(8,128)(2,1)} copy(bf16[128,128]{0,1:T(8,128)(2,1)} %bitcast.36) | data formatting | bytes 65536 | tf_op jit(solution)/shard_map/transpose | solution.py:517
  2.1 0.0 copy-done.2
  2.2 1.5 %copy_bitcast_fusion = (bf16[2,4,32,128]{3,2,1,0:T(8,128)(2,1)}, bf16[2,4,32,128]{3,2,1,0:T(8,128)(2,1)}) fusion(bf16[2,32,4,128]{3,2,1,0:T(4,128)(2,1)S(1)} %copy-done.2, bf16[2,32,4,128]{3,2,1,0:T(4,128)(2,1)} %param.6), kind=kLoop, calls=%fused_computation.1 | loop fusion | bytes 262144 | tf_op jit(solution)/shard_map/transpose | solution.py:513
  3.7 57.0 %shard_map.109 = (bf16[2,2,4,32,128]{4,3,2,1,0:T(8,128)(2,1)}, f32[32,1,8,128]{3,2,1,0:T(8,128)}, bf16[2,128,128]{2,1,0:T(8,128)(2,1)}, f32[3,40,128]{2,1,0:T(8,128)}) custom-call(bf16[2,4,32,128]{3,2,1,0:T(8,128)(2,1)} %get-tuple-element.37.mi_ref, bf16[2,4,32,128]{3,2,1,0:T(8,128)(2,1)} %get-tuple-element.36.mc_ref, bf16[27,32,32]{2,1,0:T(8,128)(2,1)} %bitcast.35, ...), custom_call_target="tpu_custom_call" | custom-call | tf_op jit(solution)/shard_map/pallas_call | solution.py:521
  60.7 0.9 %slice_bitcast_fusion.1 = (bf16[2,32,4,128]{3,1,2,0:T(8,128)(2,1)S(1)}, bf16[2,32,4,128]{3,1,2,0:T(8,128)(2,1)S(1)}) fusion(bf16[2,2,4,32,128]{4,3,2,1,0:T(8,128)(2,1)} %get-tuple-element.10), kind=kLoop, calls=%fused_computation.3 | loop fusion | bytes 262144 | tf_op jit(solution)/shard_map/transpose | solution.py:585
  61.6 0.0 copy-start.3
  61.6 0.7 %copy.27 = bf16[2,32,4,128]{3,2,1,0:T(4,128)(2,1)} copy(bf16[2,32,4,128]{3,1,2,0:T(8,128)(2,1)S(1)} %get-tuple-element.32) | data formatting | bytes 131072
  62.3 0.2 copy-done.3
  62.4 0.0 copy-start.1
  62.4 0.6 reshape.50
  63.1 0.0 copy-start
  63.1 0.7 %copy.26 = bf16[2,32,4,128]{3,2,1,0:T(4,128)(2,1)} copy(bf16[2,32,4,128]{3,1,2,0:T(8,128)(2,1)S(1)} %get-tuple-element.33) | data formatting | bytes 131072
  63.7 0.0 copy-done.1
  63.7 0.6 fusion
  64.4 0.0 copy-done
  64.4 1.0 %copy.29 = f32[864,32]{1,0:T(8,128)} copy(f32[864,32]{0,1:T(8,128)S(1)} %slice_bitcast_fusion) | data formatting | bytes 221184
  (2 shorter events, 0.0 us)
Async XLA Ops:
  0.6 1.5 %copy-start.2 = (bf16[2,32,4,128]{3,2,1,0:T(4,128)(2,1)S(1)}, bf16[2,32,4,128]{3,2,1,0:T(4,128)(2,1)}, u32[]{:S(2)}) copy-start(bf16[2,32,4,128]{3,2,1,0:T(4,128)(2,1)} %param.7) | copy-start | bytes 196612
  61.6 0.8 %copy-start.3 = (f32[3,40,128]{2,1,0:T(8,128)S(1)}, f32[3,40,128]{2,1,0:T(8,128)}, u32[]{:S(2)}) copy-start(f32[3,40,128]{2,1,0:T(8,128)} %get-tuple-element.13) | copy-start | bytes 184324
  62.4 1.3 %copy-start.1 = (bf16[2,128,128]{2,1,0:T(8,128)(2,1)S(1)}, bf16[2,128,128]{2,1,0:T(8,128)(2,1)}, u32[]{:S(2)}) copy-start(bf16[2,128,128]{2,1,0:T(8,128)(2,1)} %get-tuple-element.12) | copy-start | bytes 196612
  63.1 1.3 %copy-start = (f32[32,1,8,128]{3,2,1,0:T(8,128)S(1)}, f32[32,1,8,128]{3,2,1,0:T(8,128)}, u32[]{:S(2)}) copy-start(f32[32,1,8,128]{3,2,1,0:T(8,128)} %get-tuple-element.11) | copy-start | bytes 393220
